TPU v7x, 512 devices: a whole 4x8x8 slice. The times are simulated.
512 devices in a mesh: grp: 8 (over z_lo, x), tile: 64 (over y, z_hi, core).
Axes of the slice: x: 4, y: 8, z: 8 (z_hi: 4, z_lo: 2; z = z_hi * 2 + z_lo), core: 2. Of those that a mesh axis runs over, the one named last changes fastest.
Arguments:
- pixels: bfloat16 [512, 128, 3, 256], P(('grp', 'tile')), parts along dimension 0, may hold values from -6 to 6
- patch_weight: bfloat16 [768, 1024], P('tile'), may hold values from -0.21875 to 0.21875
- qkv_weight: bfloat16 [1024, 1536], P('tile'), may hold values from -2.0625 to 2.0625
- out_weight: bfloat16 [512, 1024], P('tile'), may hold values from -0.25 to 0.25
- reward_head: float32 [1024], replicated, may hold values from -4 to 4
- conv_weight: bfloat16 [3, 3, 48, 3], replicated, may hold values from -1.25 to 1.25
Outputs:
- rewards: float32 [512], P(('grp', 'tile')), parts along dimension 0
- act_grad: bfloat16 [512, 128, 48, 256], P('grp', 'tile'), parts along dimension 0
There are 8 independent parts, one for each index of `grp`. A program takes and returns all parts, laid end to end along the dimension named above; an argument that names none is the same for every part. Nothing has to cross between parts.
All inputs are finite; a program needn't handle non-finite values.
Results may differ from a plain program's by a relative error of at most 0.02.
Values may be sent and summed in bfloat16 or wider, within the bound.
No kernel may reach another device: no remote copies, remote signals or barrier semaphores. Data moves between devices by JAX's collectives and lax.ppermute only.
A program may use at most 64 MiB of HBM per device.

v0:
```python
import jax
import jax.numpy as jnp
from jax import lax
from jax.sharding import PartitionSpec as P

D = 1024
HEADS = 8
HEAD_DIM = 64
PATCH = 16
PDIM = 768


LOSS_SCALE = 1024.0
NORM_EPSILON = 1e-05


def extended(value, sides, width):
    for axis, dim in sides:
        devices, length = (lax.axis_size(axis), value.shape[dim])
        up = [(i, (i + 1) % devices) for i in range(devices - 1)]
        down = [(j, i) for i, j in up]
        last = lax.slice_in_dim(value, length - width, length, axis=dim)
        first = lax.slice_in_dim(value, 0, width, axis=dim)
        before = lax.ppermute(last, axis, up)
        after = lax.ppermute(first, axis, down)
        value = jnp.concatenate([before, value, after], axis=dim)
    return value


def normalize(values_in):
    average = jnp.mean(values_in, -1, keepdims=True)
    centred = values_in - average
    inverse_scale = lax.rsqrt(jnp.mean(centred * centred, -1, keepdims=True) + NORM_EPSILON)
    return (centred * inverse_scale, inverse_scale)


def norm_back(grad_in, normed, inverse_scale):
    return inverse_scale * (
        grad_in
        - jnp.mean(grad_in, -1, keepdims=True)
        - normed * jnp.mean(grad_in * normed, -1, keepdims=True)
    )


def to_patch_rows(pixels):
    frame_count, row_count, _, col_count = pixels.shape
    blocks = pixels.reshape(frame_count, row_count // PATCH, PATCH, 3, col_count // PATCH, PATCH)
    blocks = blocks.transpose(0, 1, 4, 3, 2, 5)
    return blocks.reshape(frame_count, row_count // PATCH * (col_count // PATCH), 3 * PATCH * PATCH)


def from_patch_rows(patches, row_count, col_count):
    frame_count = patches.shape[0]
    blocks = patches.reshape(frame_count, row_count // PATCH, col_count // PATCH, 3, PATCH, PATCH)
    blocks = blocks.transpose(0, 1, 4, 3, 2, 5)
    return blocks.reshape(frame_count, row_count, 3, col_count)


def attend_forward(spread, full_qkv):
    frame_count, local_count, model_width = spread.shape
    score_scale = HEAD_DIM ** (-0.5)
    first_normed, first_scale = normalize(spread.astype(jnp.float32))
    projected = jnp.dot(
        first_normed.astype(jnp.bfloat16).reshape(-1, model_width),
        full_qkv,
        preferred_element_type=jnp.float32,
    )
    projected = projected.astype(jnp.bfloat16).reshape(frame_count, local_count, 3, HEADS, HEAD_DIM)
    query_rows = projected[:, :, 0]
    key_rows = projected[:, :, 1]
    value_rows = projected[:, :, 2]
    scores = (
        jnp.einsum("iphd,jphd->phij", query_rows, key_rows, preferred_element_type=jnp.float32)
        * score_scale
    )
    attn_probs = jax.nn.softmax(scores, axis=-1)
    probs_rounded = attn_probs.astype(jnp.bfloat16)
    attended = jnp.einsum(
        "phij,jphd->iphd", probs_rounded, value_rows, preferred_element_type=jnp.float32
    )
    attended = attended.astype(jnp.bfloat16).reshape(frame_count, local_count, HEADS * HEAD_DIM)
    return (
        first_normed,
        first_scale,
        query_rows,
        key_rows,
        value_rows,
        attn_probs,
        probs_rounded,
        attended,
    )


def attend_backward(grad_spread, saved, back_qkv):
    first_normed, first_scale, query_rows, key_rows, value_rows, attn_probs, probs_rounded, _ = (
        saved
    )
    frame_count, local_count = (first_normed.shape[0], first_normed.shape[1])
    score_scale = HEAD_DIM ** (-0.5)
    grad_heads = grad_spread.reshape(frame_count, local_count, HEADS, HEAD_DIM)
    grad_probs = jnp.einsum(
        "iphd,jphd->phij", grad_heads, value_rows, preferred_element_type=jnp.float32
    )
    grad_value = jnp.einsum(
        "phij,iphd->jphd", probs_rounded, grad_heads, preferred_element_type=jnp.float32
    ).astype(jnp.bfloat16)
    row_delta = jnp.sum(attn_probs * grad_probs, -1, keepdims=True)
    grad_scores = (attn_probs * (grad_probs - row_delta) * score_scale).astype(jnp.bfloat16)
    grad_query = jnp.einsum(
        "phij,jphd->iphd", grad_scores, key_rows, preferred_element_type=jnp.float32
    ).astype(jnp.bfloat16)
    grad_key = jnp.einsum(
        "phij,iphd->jphd", grad_scores, query_rows, preferred_element_type=jnp.float32
    ).astype(jnp.bfloat16)
    grad_proj = jnp.stack([grad_query, grad_key, grad_value], 2).reshape(-1, 3 * HEADS * HEAD_DIM)
    grad_first = jnp.dot(grad_proj, back_qkv.T, preferred_element_type=jnp.float32)
    grad_first = grad_first.reshape(first_normed.shape)
    return norm_back(grad_first, first_normed, first_scale).astype(jnp.bfloat16)


def on_device(pixels, patch_weight, qkv_weight, out_weight, reward_head, conv_weight):
    local_frames, row_count, _, col_count = pixels.shape
    model_width = D
    inner_width = HEADS * HEAD_DIM
    full_patch, full_qkv, full_out = (
        lax.all_gather(patch_weight, "tile", axis=0, tiled=True),
        lax.all_gather(qkv_weight, "tile", axis=0, tiled=True),
        lax.all_gather(out_weight, "tile", axis=0, tiled=True),
    )
    patches = to_patch_rows(pixels)
    patch_count = patches.shape[1]
    spread_patches = lax.all_to_all(patches, "tile", split_axis=1, concat_axis=0, tiled=True)
    frame_count, local_count = (spread_patches.shape[0], spread_patches.shape[1])
    embedded = jnp.dot(
        spread_patches.reshape(-1, PDIM), full_patch, preferred_element_type=jnp.float32
    )
    embedded = embedded.astype(jnp.bfloat16).reshape(frame_count, local_count, model_width)
    saved = attend_forward(embedded, full_qkv)
    hidden = embedded.astype(jnp.float32) + jnp.dot(
        saved[7].reshape(-1, inner_width), full_out, preferred_element_type=jnp.float32
    ).reshape(embedded.shape)
    second_normed, second_scale = normalize(hidden)
    partial_sums = jnp.sum(jnp.sum(second_normed * reward_head, -1), -1)
    all_rewards = lax.psum(partial_sums, "tile") / patch_count
    rewards = lax.dynamic_slice_in_dim(
        all_rewards, lax.axis_index("tile") * local_frames, local_frames
    )
    frame_coeff = -LOSS_SCALE * jax.nn.sigmoid(-all_rewards)
    grad_second = frame_coeff[:, None, None] * reward_head / patch_count
    grad_hidden = norm_back(grad_second, second_normed, second_scale)
    hidden_rounded = grad_hidden.astype(jnp.bfloat16)
    back_patch, back_qkv, back_out = (
        lax.all_gather(patch_weight, "tile", axis=0, tiled=True),
        lax.all_gather(qkv_weight, "tile", axis=0, tiled=True),
        lax.all_gather(out_weight, "tile", axis=0, tiled=True),
    )
    grad_attended = jnp.dot(
        hidden_rounded.reshape(-1, model_width), back_out.T, preferred_element_type=jnp.float32
    )
    grad_attended = grad_attended.astype(jnp.bfloat16).reshape(
        hidden.shape[0], hidden.shape[1], inner_width
    )
    grad_embed = attend_backward(grad_attended, saved, back_qkv)
    grad_total = (grad_hidden + grad_embed.astype(jnp.float32)).astype(jnp.bfloat16)
    grad_patches = jnp.dot(
        grad_total.reshape(-1, model_width), back_patch.T, preferred_element_type=jnp.float32
    )
    grad_patches = grad_patches.astype(jnp.bfloat16).reshape(hidden.shape[0], hidden.shape[1], PDIM)
    home_patches = lax.all_to_all(grad_patches, "tile", split_axis=0, concat_axis=1, tiled=True)
    grad_pixels = from_patch_rows(home_patches, row_count, col_count)
    row_grad = lax.all_to_all(grad_pixels, "tile", split_axis=1, concat_axis=0, tiled=True)
    tile_rows = row_grad.shape[1]
    padded = extended(row_grad, (("tile", 1),), 1)
    padded = jnp.pad(padded, ((0, 0), (0, 0), (0, 0), (1, 1)))
    pieces = [
        padded[:, 2 - row_off : 2 - row_off + tile_rows, :, 2 - col_off : 2 - col_off + col_count]
        for row_off in range(3)
        for col_off in range(3)
    ]
    stacked = jnp.stack(pieces, 2).reshape(row_grad.shape[0], tile_rows, 27, col_count)
    kernel = conv_weight.transpose(0, 1, 3, 2).reshape(27, -1)
    act_grad = jnp.einsum(
        "fykx,kc->fycx", stacked, kernel, preferred_element_type=jnp.float32
    ).astype(jnp.bfloat16)
    return (rewards, act_grad)


def solution(mesh):
    in_specs = (
        P(("grp", "tile"), None, None, None),
        P("tile", None),
        P("tile", None),
        P("tile", None),
        P(),
        P(),
    )
    out_specs = (P(("grp", "tile")), P("grp", "tile", None, None))
    return jax.shard_map(
        on_device, mesh=mesh, in_specs=in_specs, out_specs=out_specs, check_vma=False
    )
```

profile of v0, /device:TPU:1, one launch (start us, length us, event | category | flops | bytes accessed | tf_op | source)
XLA Modules:
  0.0 508.4 jit_solution(12765785373744496446)
XLA Ops:
  8.6 2.1 reshape.213
  11.2 1.1 reshape.230
  12.8 1.8 reduce.4
  14.6 0.8 reshape.233
  15.3 17.6 %all-to-all-start = ((bf16[64,2,768]{2,1,0:T(2,128)(2,1)}), bf16[64,2,768]{2,1,0:T(2,128)(2,1)S(1)}, u32[]{:S(2)}, u32[]{:S(2)}) async-start(bf16[64,2,768]{2,1,0:T(2,128)(2,1)} %reshape.233), calls=%async_computation | async-start | bytes 393216 | tf_op jit(solution)/shard_map/all_to_all | solution.py:132
  33.7 14.1 %all-to-all-done = bf16[64,2,768]{2,1,0:T(2,128)(2,1)S(1)} async-done(((bf16[64,2,768]{2,1,0:T(2,128)(2,1)}), bf16[64,2,768]{2,1,0:T(2,128)(2,1)S(1)}, u32[]{:S(2)}, u32[]{:S(2)}) %all-to-all-start) | async-done | bytes 196640 | tf_op jit(solution)/shard_map/all_to_all | solution.py:132
  47.9 55.3 %all-gather.9.cloned.1.call-done = bf16[64,12,1024]{2,1,0:T(8,128)(2,1)} async-done(((bf16[1,12,1024]{2,1,0:T(8,128)(2,1)}), bf16[64,12,1024]{2,1,0:T(8,128)(2,1)}) %all-gather.9.cloned.1.call-update) | async-done | bytes 1572880 | tf_op jit(solution)/shard_map/all_gather | solution.py:126
  103.2 2.5 reshape.226
  107.7 81.3 %all-gather.5.cloned.1.call-done = bf16[1024,1536]{1,0:T(8,128)(2,1)} async-done(((bf16[16,1536]{1,0:T(8,128)(2,1)}), bf16[1024,1536]{1,0:T(8,128)(2,1)}) %all-gather.5.cloned.1.call-update) | async-done | bytes 3145744 | tf_op jit(solution)/shard_map/all_gather | solution.py:127
  189.0 2.5 convolution_convert_fusion
  192.0 0.9 fusion.51
  193.2 1.4 fusion.54
  195.4 76.6 %all-gather.7.cloned.1.call-done = bf16[512,1024]{1,0:T(8,128)(2,1)} async-done(((bf16[8,1024]{1,0:T(8,128)(2,1)}), bf16[512,1024]{1,0:T(8,128)(2,1)}) %all-gather.7.cloned.1.call-update) | async-done | bytes 1048592 | tf_op jit(solution)/shard_map/all_gather | solution.py:128
  272.0 1.7 fusion.55
  274.2 138.3 %psum.7 = f32[64]{0:T(128)S(1)} all-reduce(f32[64]{0:T(128)S(1)} %multiply_reduce_fusion.3), channel_id=1, replica_groups=mesh['grp'=8,'tile'=64] {'tile'}, use_global_device_ids=true, to_apply=%region_7.0 | all-reduce | flops 64 | bytes 512 | tf_op jit(solution)/shard_map/psum | solution.py:144
  414.6 1.7 convolution_convert_fusion.7
  416.8 1.1 fusion.22
  417.9 2.7 fusion.13
  420.6 2.6 fusion.14
  423.1 1.4 fusion.15
  424.8 1.3 copy.177
  426.0 1.8 dot_general.54
  427.8 3.2 fusion.50
  432.6 23.5 %all_to_all.30 = bf16[64,2,768]{2,1,0:T(2,128)(2,1)S(1)} all-to-all(bf16[64,2,768]{2,1,0:T(2,128)(2,1)S(1)} %reshape.219), channel_id=1, replica_groups=mesh['grp'=8,'tile'=64] {'tile'}, dimensions={0} | all-to-all | bytes 393216 | tf_op jit(solution)/shard_map/all_to_all | solution.py:169
  456.1 1.1 reshape.220
  457.6 1.8 reshape.231
  459.4 19.2 %all_to_all.31 = bf16[1,128,3,256]{3,2,0,1:T(4,128)(2,1)S(1)} all-to-all(bf16[1,128,3,256]{3,2,0,1:T(4,128)(2,1)S(1)} %reshape.231), channel_id=1, replica_groups=mesh['grp'=8,'tile'=64] {'tile'}, dimensions={1} | all-to-all | bytes 393216 | tf_op jit(solution)/shard_map/all_to_all | solution.py:171
  479.1 3.3 collective-permute-start
  482.4 2.1 collective-permute-start.1
  485.2 8.7 %collective-permute-done.1 = bf16[64,1,3,256]{3,1,0,2:T(2,128)(2,1)S(1)} collective-permute-done((bf16[64,1,3,256]{3,1,0,2:T(2,128)(2,1)S(1)}, bf16[64,1,3,256]{3,1,0,2:T(2,128)(2,1)S(1)}, u32[]{:S(2)}, u32[]{:S(2)}) %collective-permute-start.1) | collective-permute-done | bytes 98336 | tf_op jit(solution)/shard_map/ppermute | solution.py:25
  493.8 1.8 select_maximum_fusion
  498.8 3.1 convert_bitcast_fusion
  (82 shorter events, 16.1 us)
Async XLA Ops:
  7.2 96.0 %all-gather.9.cloned.1.call-start = ((), (), s32[]{:S(2)}) async-start(), calls=%async_computation.5 | async-start | bytes 2129920 | tf_op jit(solution)/shard_map/all_gather | solution.py:126
  7.9 181.1 %all-gather.5.cloned.1.call-start = ((), (), s32[]{:S(2)}) async-start(), calls=%async_computation.3 | async-start | bytes 3194880 | tf_op jit(solution)/shard_map/all_gather | solution.py:127
  15.3 32.4 %all-to-all-start = ((bf16[64,2,768]{2,1,0:T(2,128)(2,1)}), bf16[64,2,768]{2,1,0:T(2,128)(2,1)S(1)}, u32[]{:S(2)}, u32[]{:S(2)}) async-start(bf16[64,2,768]{2,1,0:T(2,128)(2,1)} %reshape.233), calls=%async_computation | async-start | bytes 393216 | tf_op jit(solution)/shard_map/all_to_all | solution.py:132
  32.9 239.1 %all-gather.7.cloned.1.call-start = ((), (), s32[]{:S(2)}) async-start(), calls=%async_computation.4 | async-start | bytes 1064960 | tf_op jit(solution)/shard_map/all_gather | solution.py:128
  194.6 0.6 copy-start.10
  194.6 77.4 %copy-start.9 = (f32[2,8,64,64]{2,3,1,0:T(8,128)}, f32[2,8,64,64]{2,3,1,0:T(8,128)S(1)}, u32[]{:S(2)}) copy-start(f32[2,8,64,64]{2,3,1,0:T(8,128)S(1)} %get-tuple-element.16) | copy-start | bytes 786436
  195.4 78.5 %copy-start.5 = (f32[1024]{0:T(1024)S(1)}, f32[1024]{0:T(1024)}, u32[]{:S(2)}) copy-start(f32[1024]{0:T(1024)} %param.10) | copy-start | bytes 12292
  413.3 0.7 copy-start
  416.8 3.7 copy-start.2
  416.8 3.7 copy-start.11
  423.1 1.4 copy-start.3
  423.1 1.4 copy-start.4
  424.7 3.0 copy-start.7
  427.8 3.2 copy-start.1
  457.6 26.9 %copy-start.6 = (bf16[3,3,48,3]{2,3,1,0:T(4,128)(2,1)S(1)}, bf16[3,3,48,3]{2,3,1,0:T(4,128)(2,1)}, u32[]{:S(2)}) copy-start(bf16[3,3,48,3]{2,3,1,0:T(4,128)(2,1)} %param.11) | copy-start | bytes 7780
  457.6 26.9 %copy-start.8 = (f32[64]{0:T(128)S(1)}, f32[64]{0:T(128)}, u32[]{:S(2)}) copy-start(f32[64]{0:T(128)} %get-tuple-element.12) | copy-start | bytes 772
  479.1 6.1 %collective-permute-start = (bf16[64,1,3,256]{3,1,0,2:T(2,128)(2,1)S(1)}, bf16[64,1,3,256]{3,1,0,2:T(2,128)(2,1)S(1)}, u32[]{:S(2)}, u32[]{:S(2)}) collective-permute-start(bf16[64,1,3,256]{3,1,0,2:T(2,128)(2,1)S(1)} %get-tuple-element.7), channel_id=1, source_target_pairs={{0,1},{1,2},{2,3},{3,4},{4,5},{5,6},{6,7},{7,8},{8,9},{9,10},{10,1... | collective-permute-start | bytes 294920 | tf_op jit(solution)/shard_map/ppermute | solution.py:24
  482.4 11.5 %collective-permute-start.1 = (bf16[64,1,3,256]{3,1,0,2:T(2,128)(2,1)S(1)}, bf16[64,1,3,256]{3,1,0,2:T(2,128)(2,1)S(1)}, u32[]{:S(2)}, u32[]{:S(2)}) collective-permute-start(bf16[64,1,3,256]{3,1,0,2:T(2,128)(2,1)S(1)} %get-tuple-element.8), channel_id=1, source_target_pairs={{1,0},{2,1},{3,2},{4,3},{5,4},{6,5},{7,6},{8,7},{9,8},{10,9},{11,1... | collective-permute-start | bytes 294920 | tf_op jit(solution)/shard_map/ppermute | solution.py:25
Sparse Core Ops, SparseCore 0:
  11.3 91.8 all-gather.8
  106.5 82.4 all-gather.4
  192.3 79.6 all-gather.6
where the time goes:
time: 509 us; the launch traced here: 508 us
  waiting for transfers between devices  238 us (47%)
  blocking collectives  181 us (36%)
  starting transfers between devices  23.1 us (5%)
  matrix products  22.6 us (4%)
  local copies, waits for them, and re-layouts  22.4 us (4%)
  between operations  14.2 us (3%)
  other arithmetic  7.14 us (1%)
    psum x1, blocking collectives, on_device(): all_rewards = lax.psum(partial_sums, 'tile') / patch_count  138 us
    all_gather x1, waiting for transfers between devices, on_device(): lax.all_gather(qkv_weight, 'tile', axis=0, tiled=True)  81.3 us
    all_gather x1, waiting for transfers between devices, on_device(): lax.all_gather(out_weight, 'tile', axis=0, tiled=True)  76.6 us
    all_gather x1, waiting for transfers between devices, on_device(): lax.all_gather(patch_weight, 'tile', axis=0, tiled=True)  55.3 us
    all_to_all x1, blocking collectives, on_device(): lax.all_to_all(grad_patches, 'tile', split_axis=0, concat_axis=1, tiled=T...  23.5 us
    all_to_all x1, blocking collectives, on_device(): lax.all_to_all(grad_pixels, 'tile', split_axis=1, concat_axis=0, tiled=True)  19.2 us
    all_to_all x1, starting transfers between devices, on_device(): lax.all_to_all(patches, 'tile', split_axis=1, concat_axis=0, tiled=True)  17.6 us
    all_to_all x1, waiting for transfers between devices, on_device(): lax.all_to_all(patches, 'tile', split_axis=1, concat_axis=0, tiled=True)  14.1 us
  transfers between devices with their start and end apart: 6, of which 5 were waited for; matrix products, arithmetic and copies ran while one was open for 3% of the time, Pallas kernels for 0%

commit v1 on v0

--- a/solution.py
+++ b/solution.py
@@ -1,6 +1,7 @@
 import jax
 import jax.numpy as jnp
 from jax import lax
+from jax.sharding import Mesh
 from jax.sharding import PartitionSpec as P
 
 D = 1024
@@ -9,6 +10,10 @@
 PATCH = 16
 PDIM = 768
 
+
+GRP = ("zl", "x")
+TILE = ("y", "zh", "core")
+ROW = ("zh", "core")
 
 LOSS_SCALE = 1024.0
 NORM_EPSILON = 1e-05
@@ -118,18 +123,35 @@
     return norm_back(grad_first, first_normed, first_scale).astype(jnp.bfloat16)
 
 
+def gather_weights(patch_weight, qkv_weight, out_weight):
+    half = out_weight.shape[1] // 2
+    rows = qkv_weight.shape[0]
+    packed = jnp.concatenate(
+        [
+            jnp.pad(patch_weight, ((0, rows - patch_weight.shape[0]), (0, 0))),
+            qkv_weight,
+            jnp.concatenate([out_weight[:, :half], out_weight[:, half:]], 0),
+        ],
+        1,
+    )
+    full = lax.all_gather(packed, TILE, axis=0, tiled=True)
+    width = patch_weight.shape[1]
+    inner = qkv_weight.shape[1]
+    full_patch = full[:, :width].reshape(-1, rows, width)[:, : patch_weight.shape[0]]
+    full_qkv = full[:, width : width + inner]
+    full_out = full[:, width + inner :].reshape(-1, 2, out_weight.shape[0], half)
+    full_out = full_out.transpose(0, 2, 1, 3)
+    return full_patch.reshape(-1, width), full_qkv, full_out.reshape(-1, 2 * half)
+
+
 def on_device(pixels, patch_weight, qkv_weight, out_weight, reward_head, conv_weight):
     local_frames, row_count, _, col_count = pixels.shape
     model_width = D
     inner_width = HEADS * HEAD_DIM
-    full_patch, full_qkv, full_out = (
-        lax.all_gather(patch_weight, "tile", axis=0, tiled=True),
-        lax.all_gather(qkv_weight, "tile", axis=0, tiled=True),
-        lax.all_gather(out_weight, "tile", axis=0, tiled=True),
-    )
+    full_patch, full_qkv, full_out = gather_weights(patch_weight, qkv_weight, out_weight)
     patches = to_patch_rows(pixels)
     patch_count = patches.shape[1]
-    spread_patches = lax.all_to_all(patches, "tile", split_axis=1, concat_axis=0, tiled=True)
+    spread_patches = lax.all_to_all(patches, TILE, split_axis=1, concat_axis=0, tiled=True)
     frame_count, local_count = (spread_patches.shape[0], spread_patches.shape[1])
     embedded = jnp.dot(
         spread_patches.reshape(-1, PDIM), full_patch, preferred_element_type=jnp.float32
@@ -141,36 +163,38 @@
     ).reshape(embedded.shape)
     second_normed, second_scale = normalize(hidden)
     partial_sums = jnp.sum(jnp.sum(second_normed * reward_head, -1), -1)
-    all_rewards = lax.psum(partial_sums, "tile") / patch_count
+    copies = jnp.broadcast_to(partial_sums, (frame_count // local_frames, frame_count))
+    everyone = lax.all_to_all(copies, TILE, split_axis=0, concat_axis=0, tiled=True)
+    all_rewards = jnp.sum(everyone, 0) / patch_count
     rewards = lax.dynamic_slice_in_dim(
-        all_rewards, lax.axis_index("tile") * local_frames, local_frames
+        all_rewards, lax.axis_index(TILE) * local_frames, local_frames
     )
     frame_coeff = -LOSS_SCALE * jax.nn.sigmoid(-all_rewards)
     grad_second = frame_coeff[:, None, None] * reward_head / patch_count
     grad_hidden = norm_back(grad_second, second_normed, second_scale)
     hidden_rounded = grad_hidden.astype(jnp.bfloat16)
-    back_patch, back_qkv, back_out = (
-        lax.all_gather(patch_weight, "tile", axis=0, tiled=True),
-        lax.all_gather(qkv_weight, "tile", axis=0, tiled=True),
-        lax.all_gather(out_weight, "tile", axis=0, tiled=True),
-    )
     grad_attended = jnp.dot(
-        hidden_rounded.reshape(-1, model_width), back_out.T, preferred_element_type=jnp.float32
+        hidden_rounded.reshape(-1, model_width), full_out.T, preferred_element_type=jnp.float32
     )
     grad_attended = grad_attended.astype(jnp.bfloat16).reshape(
         hidden.shape[0], hidden.shape[1], inner_width
     )
-    grad_embed = attend_backward(grad_attended, saved, back_qkv)
+    grad_embed = attend_backward(grad_attended, saved, full_qkv)
     grad_total = (grad_hidden + grad_embed.astype(jnp.float32)).astype(jnp.bfloat16)
     grad_patches = jnp.dot(
-        grad_total.reshape(-1, model_width), back_patch.T, preferred_element_type=jnp.float32
-    )
-    grad_patches = grad_patches.astype(jnp.bfloat16).reshape(hidden.shape[0], hidden.shape[1], PDIM)
-    home_patches = lax.all_to_all(grad_patches, "tile", split_axis=0, concat_axis=1, tiled=True)
-    grad_pixels = from_patch_rows(home_patches, row_count, col_count)
-    row_grad = lax.all_to_all(grad_pixels, "tile", split_axis=1, concat_axis=0, tiled=True)
-    tile_rows = row_grad.shape[1]
-    padded = extended(row_grad, (("tile", 1),), 1)
+        grad_total.reshape(-1, model_width), full_patch.T, preferred_element_type=jnp.float32
+    )
+    sharers = lax.axis_size(ROW)
+    tile_rows = PATCH // sharers
+    grad_rows = grad_patches.astype(jnp.bfloat16).reshape(
+        frame_count, local_count, 3, sharers, tile_rows, PATCH
+    )
+    grad_rows = grad_rows.transpose(3, 0, 4, 2, 1, 5).reshape(
+        sharers, frame_count, tile_rows, 3, local_count * PATCH
+    )
+    row_grad = lax.all_to_all(grad_rows, ROW, split_axis=0, concat_axis=0, tiled=True)
+    row_grad = row_grad.transpose(1, 2, 3, 0, 4).reshape(frame_count, tile_rows, 3, col_count)
+    padded = extended(row_grad, ((TILE, 1),), 1)
     padded = jnp.pad(padded, ((0, 0), (0, 0), (0, 0), (1, 1)))
     pieces = [
         padded[:, 2 - row_off : 2 - row_off + tile_rows, :, 2 - col_off : 2 - col_off + col_count]
@@ -186,15 +210,16 @@
 
 
 def solution(mesh):
+    axes = Mesh(mesh.devices.reshape(2, 4, 8, 4, 2), GRP + TILE)
     in_specs = (
-        P(("grp", "tile"), None, None, None),
-        P("tile", None),
-        P("tile", None),
-        P("tile", None),
+        P(GRP + TILE, None, None, None),
+        P(TILE, None),
+        P(TILE, None),
+        P(TILE, None),
         P(),
         P(),
     )
-    out_specs = (P(("grp", "tile")), P("grp", "tile", None, None))
+    out_specs = (P(GRP + TILE), P(GRP, TILE, None, None))
     return jax.shard_map(
-        on_device, mesh=mesh, in_specs=in_specs, out_specs=out_specs, check_vma=False
-    )
+        on_device, mesh=axes, in_specs=in_specs, out_specs=out_specs, check_vma=False
+    )

time: 509 us -> 224 us (0.44)
  waiting for transfers between devices: 238 us -> 84.8 us
  blocking collectives: 181 us -> 44.1 us
  local copies, waits for them, and re-layouts: 22.4 us -> 35.7 us
  starting transfers between devices: 23.1 us -> 13.6 us
    all_gather x3 -> x1, waiting for transfers between devices: 213 us -> 66.4 us  [gather_weights(): full = lax.all_gather(packed, TILE, axis=0, tiled=True)]
    psum x1 -> x0, blocking collectives: 138 us -> none  [on_device(): all_rewards = lax.psum(partial_sums, 'tile') / patch_count]
    all_to_all x1, starting transfers between devices: 17.6 us -> 7.5 us  [on_device(): lax.all_to_all(copies, TILE, split_axis=0, concat_axis=0, tiled=True)]
    slice x0 -> x3, local copies, waits for them, and re-layouts: none -> 5.09 us  [the longest x1 3.08 us: gather_weights(): full[:, :width].reshape(-1, rows, width)[:, :patch_weight.shape[0]]]
  transfers between devices with their start and end apart: 6 -> 4, of which waited for: 5 -> 4; matrix products, arithmetic and copies ran while one was open for 3% -> 3% of each run, Pallas kernels for 0% -> 0%
where the time goes in v1:
time: 224 us; the launch traced here: 223 us
  waiting for transfers between devices  84.8 us (38%)
  blocking collectives  44.1 us (20%)
  local copies, waits for them, and re-layouts  35.7 us (16%)
  matrix products  21.3 us (10%)
  between operations  14.5 us (6%)
  starting transfers between devices  13.6 us (6%)
  other arithmetic  8.83 us (4%)
    all_gather x1, waiting for transfers between devices, gather_weights(): full = lax.all_gather(packed, TILE, axis=0, tiled=True)  66.4 us
    all_to_all x1, blocking collectives, on_device(): lax.all_to_all(patches, TILE, split_axis=1, concat_axis=0, tiled=True)  32.5 us
    all_to_all x1, blocking collectives, on_device(): lax.all_to_all(grad_rows, ROW, split_axis=0, concat_axis=0, tiled=True)  11.6 us
    all_to_all x1, waiting for transfers between devices, on_device(): lax.all_to_all(copies, TILE, split_axis=0, concat_axis=0, tiled=True)  10.8 us
    unnamed x40, local copies, waits for them, and re-layouts  7.61 us
    all_to_all x1, starting transfers between devices, on_device(): lax.all_to_all(copies, TILE, split_axis=0, concat_axis=0, tiled=True)  7.5 us
    ppermute x1, waiting for transfers between devices, extended(): after = lax.ppermute(first, axis, down)  7.5 us
  transfers between devices with their start and end apart: 4, of which 4 were waited for; matrix products, arithmetic and copies ran while one was open for 3% of the time, Pallas kernels for 0%

profile of v1, /device:TPU:1, one launch (start us, length us, event | category | flops | bytes accessed | tf_op | source)
XLA Modules:
  0.0 222.8 jit_solution(8318940242061947448)
XLA Ops:
  7.9 1.5 fusion.55
  9.4 2.1 reshape.235
  11.9 1.1 reshape.252
  13.5 1.8 reduce.7
  15.4 32.5 %all_to_all.20 = bf16[64,2,768]{2,1,0:T(2,128)(2,1)S(1)} all-to-all(bf16[64,2,768]{2,1,0:T(2,128)(2,1)S(1)} %reshape.254), channel_id=1, replica_groups=mesh['zl'=2,'x'=4,'y'=8,'zh'=4,'core'=2] {'y','zh','core'}, dimensions={0} | all-to-all | bytes 393216 | tf_op jit(solution)/shard_map/all_to_all | solution.py:154
  48.1 66.4 %all-gather.2.cloned.1.call-done = bf16[1024,3072]{1,0:T(8,128)(2,1)} async-done(((bf16[16,3072]{1,0:T(8,128)(2,1)}), bf16[1024,3072]{1,0:T(8,128)(2,1)}) %all-gather.2.cloned.1.call-update) | async-done | bytes 6291472 | tf_op jit(solution)/shard_map/all_gather | solution.py:137
  114.5 3.1 %slice.82 = bf16[1024,1024]{1,0:T(8,128)(2,1)} slice(bf16[1024,3072]{1,0:T(8,128)(2,1)} %all-gather.2.cloned.1.call-done), slice={[0:1024], [0:1024]} | slice | bytes 4194304 | tf_op jit(solution)/shard_map/slice | solution.py:140
  117.6 2.5 %reshape.234 = bf16[768,1024]{1,0:T(8,128)(2,1)S(1)} reshape(bf16[64,12,1024]{2,1,0:T(8,128)(2,1)} %bitcast.142) | data formatting | bytes 3145728 | tf_op jit(solution)/shard_map/reshape | solution.py:144
  120.8 2.5 %fusion.7 = bf16[128,1536]{1,0:T(8,128)(2,1)S(1)} fusion(bf16[1024,3072]{1,0:T(8,128)(2,1)} %all-gather.2.cloned.1.call-done, f32[1024,128]{0,1:T(8,128)S(1)} %get-tuple-element.16, f32[128]{0:T(128)S(1)} %add_rsqrt_fusion.1, f32[128]{0:T(128)S(1)} %broadcast_multiply_fusion.6), kind=kOutput, calls=%fused_computation.10 | convolution fusion | flops 403243008 | bytes 4064256 | tf_op jit(solution)/shard_map/dot_general | solution.py:68
  124.9 1.1 reshape.248
  126.0 1.3 fusion.68
  128.1 1.3 slice.88
  131.0 7.5 %all-to-all-start.1 = ((f32[64,1,64]{2,1,0:T(1,128)}), f32[64,1,64]{2,1,0:T(1,128)S(1)}, u32[]{:S(2)}, u32[]{:S(2)}) async-start(f32[64,1,64]{2,1,0:T(1,128)} %broadcast_in_dim.2), calls=%async_computation.1 | async-start | bytes 65536 | tf_op jit(solution)/shard_map/all_to_all | solution.py:167
  139.6 10.8 %all-to-all-done.1 = f32[64,1,64]{2,1,0:T(1,128)S(1)} async-done(((f32[64,1,64]{2,1,0:T(1,128)}), f32[64,1,64]{2,1,0:T(1,128)S(1)}, u32[]{:S(2)}, u32[]{:S(2)}) %all-to-all-start.1) | async-done | bytes 16416 | tf_op jit(solution)/shard_map/all_to_all | solution.py:167
  153.3 1.5 convolution_convert_fusion.6
  155.2 1.2 fusion.42
  156.5 2.3 %fusion.19 = bf16[64,2,1,8,64]{0,4,3,1,2:T(8,128)(2,1)} fusion(f32[2,8,64,64]{2,3,1,0:T(8,128)S(1)} %fusion.42, bf16[64,2,1,8,64]{4,3,2,1,0:T(8,128)(2,1)} %get-tuple-element.4, f32[2,8,64,64]{2,3,1,0:T(8,128)} %copy-done.11, f32[2,8,64]{2,1,0:T(8,128)} %copy-done.12), kind=kOutput, calls=%fused_computation.29 | convolution fusion | flops 8913983 | bytes 790528 | tf_op jit(solution)/shard_map/phij,jphd->iphd/dot_general | solution.py:114
  158.8 2.3 %fusion.20 = bf16[64,2,1,8,64]{0,4,3,1,2:T(8,128)(2,1)} fusion(f32[2,8,64,64]{2,3,1,0:T(8,128)S(1)} %fusion.42, bf16[64,2,1,8,64]{4,3,2,1,0:T(8,128)(2,1)S(1)} %copy-done.6, f32[2,8,64,64]{2,3,1,0:T(8,128)} %copy-done.11, f32[2,8,64]{2,1,0:T(8,128)} %copy-done.12), kind=kOutput, calls=%fused_computation.30 | convolution fusion | flops 8913983 | bytes 790528 | tf_op jit(solution)/shard_map/phij,iphd->jphd/dot_general | solution.py:117
  161.1 1.4 fusion.21
  162.5 1.2 pad_maximum_fusion
  163.7 1.3 copy.158
  165.0 1.8 dot_general.54
  166.8 3.2 %fusion.63 = (f32[64,2]{0,1:T(2,128)S(1)}, f32[64,2]{0,1:T(2,128)S(1)}, f32[64,2,1024]{2,0,1:T(8,128)S(1)}) fusion(f32[64,2]{0,1:T(2,128)S(1)} %copy.148, f32[64,2]{0,1:T(2,128)S(1)} %copy-done.9, f32[64,2,1024]{2,1,0:T(2,128)S(1)} %copy-done.1, bf16[64,2,1536]{2,0,1:T(8,128)(2,1)S(1)} %dot_general.54, bf16[1024,3072]{1,0:T(8,128)(2,1)} %all-gather.2.cloned.1.call-done), kind=kOutput, calls=%fused_computation.111 | convolution fusion | flops 403308288 | bytes 4589568 | tf_op jit(solution)/shard_map/dot_general | solution.py:121
  171.4 1.2 reshape.243
  172.6 1.8 copy.162
  174.7 11.6 %all_to_all.21 = bf16[8,2,6144]{2,1,0:T(2,128)(2,1)S(1)} all-to-all(bf16[8,2,6144]{2,1,0:T(2,128)(2,1)S(1)} %reshape.256), channel_id=1, replica_groups=mesh['zl'=2,'x'=4,'y'=8,'zh'=4,'core'=2] {'zh','core'}, dimensions={0} | all-to-all | bytes 393216 | tf_op jit(solution)/shard_map/all_to_all | solution.py:195
  186.7 4.1 %collective-permute-start = (bf16[64,1,3,256]{0,3,2,1:T(8,128)(2,1)S(1)}, bf16[64,1,3,256]{0,3,2,1:T(8,128)(2,1)S(1)}, u32[]{:S(2)}, u32[]{:S(2)}) collective-permute-start(bf16[64,1,3,256]{0,3,2,1:T(8,128)(2,1)S(1)} %get-tuple-element.7), channel_id=1, source_target_pairs={{0,1},{1,2},{2,3},{3,4},{4,5},{5,6},{6,7},{7,8},{8,9},{9,10},{10,1... | collective-permute-start | bytes 294920 | tf_op jit(solution)/shard_map/ppermute | solution.py:29
  190.8 1.9 collective-permute-start.1
  193.5 7.5 %collective-permute-done.1 = bf16[64,1,3,256]{0,3,2,1:T(8,128)(2,1)S(1)} collective-permute-done((bf16[64,1,3,256]{0,3,2,1:T(8,128)(2,1)S(1)}, bf16[64,1,3,256]{0,3,2,1:T(8,128)(2,1)S(1)}, u32[]{:S(2)}, u32[]{:S(2)}) %collective-permute-start.1) | collective-permute-done | bytes 98336 | tf_op jit(solution)/shard_map/ppermute | solution.py:30
  203.7 0.9 fusion.37
  208.6 3.5 %copy.165 = bf16[64,2,9,3,256]{4,0,3,2,1:T(8,128)(2,1)S(1)} copy(bf16[64,2,9,3,256]{0,4,3,1,2:T(8,128)(2,1)} %fusion.32) | data formatting | bytes 3538944 | tf_op jit(solution)/shard_map/stack | solution.py:204
  212.1 3.9 %convert_bitcast_fusion = bf16[64,2,48,256]{3,2,1,0:T(8,128)(2,1)} fusion(bf16[64,2,27,256]{3,0,2,1:T(8,128)(2,1)S(1)} %bitcast.141, bf16[27,48,1,1]{1,0,2,3:T(8,128)(2,1)S(1)} %reshape.251), kind=kOutput, calls=%fused_computation.4 | convolution fusion | flops 86507520 | bytes 4917792 | tf_op jit(solution)/shard_map/fykx,kc->fycx/dot_general | solution.py:206
  (87 shorter events, 20.4 us)
Async XLA Ops:
  7.2 107.3 %all-gather.2.cloned.1.call-start = ((), (), s32[]{:S(2)}) async-start(), calls=%async_computation.3 | async-start | bytes 6389760 | tf_op jit(solution)/shard_map/all_gather | solution.py:137
  124.6 4.8 %copy-start.5 = (bf16[64,2,1,8,64]{4,3,2,1,0:T(8,128)(2,1)}, bf16[64,2,1,8,64]{4,3,2,1,0:T(8,128)(2,1)S(1)}, u32[]{:S(2)}) copy-start(bf16[64,2,1,8,64]{4,3,2,1,0:T(8,128)(2,1)S(1)} %get-tuple-element.6) | copy-start | bytes 393220
  124.9 2.4 %copy-start.4 = (bf16[64,2,1,8,64]{0,4,3,1,2:T(8,128)(2,1)}, bf16[64,2,1,8,64]{0,4,3,1,2:T(8,128)(2,1)S(1)}, u32[]{:S(2)}) copy-start(bf16[64,2,1,8,64]{0,4,3,1,2:T(8,128)(2,1)S(1)} %copy.177) | copy-start | bytes 393220
  127.3 0.6 copy-start.12
  127.3 2.1 copy-start.11
  127.3 2.1 copy-start
  127.9 2.3 %copy-start.7 = (f32[1024]{0:T(1024)S(1)}, f32[1024]{0:T(1024)}, u32[]{:S(2)}) copy-start(f32[1024]{0:T(1024)} %param.10) | copy-start | bytes 12292
  131.0 19.3 %all-to-all-start.1 = ((f32[64,1,64]{2,1,0:T(1,128)}), f32[64,1,64]{2,1,0:T(1,128)S(1)}, u32[]{:S(2)}, u32[]{:S(2)}) async-start(f32[64,1,64]{2,1,0:T(1,128)} %broadcast_in_dim.2), calls=%async_computation.1 | async-start | bytes 65536 | tf_op jit(solution)/shard_map/all_to_all | solution.py:167
  151.2 0.7 copy-start.2
  153.3 5.5 %copy-start.6 = (bf16[64,2,1,8,64]{4,3,2,1,0:T(8,128)(2,1)S(1)}, bf16[64,2,1,8,64]{4,3,2,1,0:T(8,128)(2,1)}, u32[]{:S(2)}) copy-start(bf16[64,2,1,8,64]{4,3,2,1,0:T(8,128)(2,1)} %copy-done.5) | copy-start | bytes 393220
  155.2 5.9 %copy-start.13 = (f32[2,8,64]{2,1,0:T(8,128)S(1)}, f32[2,8,64]{2,1,0:T(8,128)}, u32[]{:S(2)}) copy-start(f32[2,8,64]{2,1,0:T(8,128)} %copy-done.12) | copy-start | bytes 12292
  161.1 5.7 %copy-start.1 = (f32[64,2,1024]{2,1,0:T(2,128)S(1)}, f32[64,2,1024]{2,1,0:T(2,128)}, u32[]{:S(2)}) copy-start(f32[64,2,1024]{2,1,0:T(2,128)} %reshape.248) | copy-start | bytes 1572868
  161.1 5.7 %copy-start.9 = (f32[64,2]{0,1:T(2,128)S(1)}, f32[64,2]{0,1:T(2,128)}, u32[]{:S(2)}) copy-start(f32[64,2]{0,1:T(2,128)} %copy.159) | copy-start | bytes 1540
  165.0 5.0 %copy-start.3 = (f32[64,1024]{1,0:T(8,128)S(1)}, f32[64,1024]{1,0:T(8,128)}, u32[]{:S(2)}) copy-start(f32[64,1024]{1,0:T(8,128)} %copy-done.2) | copy-start | bytes 786436
  171.4 21.3 %copy-start.8 = (bf16[3,3,48,3]{2,3,1,0:T(4,128)(2,1)S(1)}, bf16[3,3,48,3]{2,3,1,0:T(4,128)(2,1)}, u32[]{:S(2)}) copy-start(bf16[3,3,48,3]{2,3,1,0:T(4,128)(2,1)} %param.11) | copy-start | bytes 7780
  171.4 21.4 %copy-start.10 = (f32[64]{0:T(128)S(1)}, f32[64]{0:T(128)}, u32[]{:S(2)}) copy-start(f32[64]{0:T(128)} %get-tuple-element.14) | copy-start | bytes 772
  186.7 6.7 %collective-permute-start = (bf16[64,1,3,256]{0,3,2,1:T(8,128)(2,1)S(1)}, bf16[64,1,3,256]{0,3,2,1:T(8,128)(2,1)S(1)}, u32[]{:S(2)}, u32[]{:S(2)}) collective-permute-start(bf16[64,1,3,256]{0,3,2,1:T(8,128)(2,1)S(1)} %get-tuple-element.7), channel_id=1, source_target_pairs={{0,1},{1,2},{2,3},{3,4},{4,5},{5,6},{6,7},{7,8},{8,9},{9,10},{10,1... | collective-permute-start | bytes 294920 | tf_op jit(solution)/shard_map/ppermute | solution.py:29
  190.8 10.1 %collective-permute-start.1 = (bf16[64,1,3,256]{0,3,2,1:T(8,128)(2,1)S(1)}, bf16[64,1,3,256]{0,3,2,1:T(8,128)(2,1)S(1)}, u32[]{:S(2)}, u32[]{:S(2)}) collective-permute-start(bf16[64,1,3,256]{0,3,2,1:T(8,128)(2,1)S(1)} %get-tuple-element.8), channel_id=1, source_target_pairs={{1,0},{2,1},{3,2},{4,3},{5,4},{6,5},{7,6},{8,7},{9,8},{10,9},{11,1... | collective-permute-start | bytes 294920 | tf_op jit(solution)/shard_map/ppermute | solution.py:30
Sparse Core Ops, SparseCore 0:
  11.9 102.6 all-gather.1

commit v2 on v1

v2 whole, which is shorter than its diff:
```python
import jax
import jax.numpy as jnp
from jax import lax
from jax.experimental import pallas as pl
from jax.experimental.pallas import tpu as pltpu
from jax.sharding import Mesh
from jax.sharding import PartitionSpec as P

D = 1024
HEADS = 8
HEAD_DIM = 64
PATCH = 16
PDIM = 768
INNER = HEADS * HEAD_DIM
SLOT = 16
PADDED = 1024
FRAMES = 64
PATCHES = 128
ROWS = 128
IMAGE_W = 256

GRP = ("zl", "x")
TILE = ("y", "zh", "core")
ROW = ("zh", "core")

LOSS_SCALE = 1024.0
NORM_EPSILON = 1e-05
F32 = jnp.float32
BF16 = jnp.bfloat16


def iota(shape, dim):
    return lax.broadcasted_iota(jnp.int32, shape, dim)


def dot(a, b):
    return lax.dot_general(a, b, (((1,), (0,)), ((), ())), preferred_element_type=F32)


def dot_t(a, b):
    return lax.dot_general(a, b, (((1,), (1,)), ((), ())), preferred_element_type=F32)


def t_dot(a, b):
    return lax.dot_general(a, b, (((0,), (0,)), ((), ())), preferred_element_type=F32)


def one_hot(condition):
    return jnp.where(condition, 1.0, 0.0).astype(F32).astype(BF16)


def normalize(values_in):
    centred = values_in - jnp.mean(values_in, -1, keepdims=True)
    inverse_scale = lax.rsqrt(jnp.mean(centred * centred, -1, keepdims=True) + NORM_EPSILON)
    return centred * inverse_scale, inverse_scale


def norm_back(grad_in, normed, inverse_scale):
    return inverse_scale * (
        grad_in
        - jnp.mean(grad_in, -1, keepdims=True)
        - normed * jnp.mean(grad_in * normed, -1, keepdims=True)
    )


def weight_copies(packed, target, sems, first, low, width):
    copies = []
    for core in range(2):
        for zh in range(4):
            copies.append(
                pltpu.make_async_copy(
                    packed.at[:, core, zh, :, pl.ds(low, width)],
                    target.at[:, zh, core],
                    sems.at[first + core * 4 + zh],
                )
            )
    return copies


def start_all(copies):
    for copy in copies:
        copy.start()


def wait_all(copies):
    for copy in copies:
        copy.wait()


def spread_kernel(patches_ref, out_ref, select_ref):
    to_row = iota((ROWS, ROWS), 0)
    from_row = iota((ROWS, ROWS), 1)
    order = one_hot(from_row == 2 * (to_row & (FRAMES - 1)) + (to_row >> 6))
    ordered = dot(order, patches_ref[...]).astype(BF16)
    slot = iota((PDIM, PADDED), 1)
    place = one_hot(
        ((slot & 15) < 12) & (iota((PDIM, PADDED), 0) == 12 * (slot >> 4) + (slot & 15))
    )
    out_ref[...] = dot(ordered, place).astype(BF16)
    slot = iota((PDIM, PADDED), 1)
    value = 12 * (slot >> 4) + (slot & 15)
    row = (value >> 4) & 15
    target = (row >> 1) * 96 + (row & 1) * 48 + (value >> 8) * 16 + (value & 15)
    select_ref[...] = one_hot(((slot & 15) < 12) & (iota((PDIM, PADDED), 0) == target))


def half_mask():
    return iota((ROWS, 2 * HEAD_DIM), 1) < HEAD_DIM


def pick(condition, value):
    return jnp.where(condition, value.astype(F32), 0.0).astype(BF16)


def forward_kernel(
    patches_ref,
    packed_ref,
    head_ref,
    normed_ref,
    scale_ref,
    proj_ref,
    probs_ref,
    second_ref,
    second_scale_ref,
    out_weight_ref,
    sums_ref,
    patch_w,
    qkv_w,
    out_w,
    sems,
):
    patch_copies = weight_copies(packed_ref, patch_w, sems, 0, 0, D)
    qkv_copies = weight_copies(packed_ref, qkv_w, sems, 8, D, 3 * INNER)
    out_copies = weight_copies(packed_ref, out_w, sems, 16, D + 3 * INNER, D // 2)
    start_all(patch_copies + qkv_copies + out_copies)
    wait_all(patch_copies)
    embedded = dot(patches_ref[...], patch_w[...].reshape(PADDED, D)).astype(BF16).astype(F32)
    normed, scale = normalize(embedded)
    normed_ref[...] = normed
    scale_ref[...] = jnp.broadcast_to(scale, (ROWS, 128))
    wait_all(qkv_copies)
    proj_ref[...] = dot(normed.astype(BF16), qkv_w[...].reshape(D, 3 * INNER)).astype(BF16)
    wait_all(out_copies)
    halves = out_w[...].reshape(64, SLOT, D // 2).astype(F32).reshape(64, 2, SLOT // 2, D // 2)
    for half in range(2):
        out_weight_ref[:, half * (D // 2) : (half + 1) * (D // 2)] = (
            halves[:, half].reshape(INNER, D // 2).astype(BF16)
        )
    same_patch = (iota((ROWS, ROWS), 0) >> 6) == (iota((ROWS, ROWS), 1) >> 6)
    low = half_mask()
    attended = []
    for pair in range(HEADS // 2):
        at = pair * 2 * HEAD_DIM
        query = proj_ref[:, at : at + 128]
        key = proj_ref[:, INNER + at : INNER + at + 128]
        value = proj_ref[:, 2 * INNER + at : 2 * INNER + at + 128]
        parts = []
        for side in range(2):
            mine = low if side == 0 else jnp.logical_not(low)
            scores = dot_t(pick(mine, query), key) * HEAD_DIM ** (-0.5)
            scores = jnp.where(same_patch, scores, -1e30)
            weights = jnp.exp(scores - jnp.max(scores, -1, keepdims=True))
            probs = weights / jnp.sum(weights, -1, keepdims=True)
            probs_ref[2 * pair + side] = probs
            parts.append(dot(probs.astype(BF16), value))
        attended.append(jnp.where(low, parts[0], parts[1]).astype(BF16))
    hidden = embedded + dot(jnp.concatenate(attended, 1), out_weight_ref[...])
    second, second_scale = normalize(hidden)
    second_ref[...] = second
    second_scale_ref[...] = jnp.broadcast_to(second_scale, (ROWS, 128))
    column = jnp.sum(second * head_ref[0:1, :], -1, keepdims=True)
    on_diagonal = iota((ROWS, ROWS), 0) == iota((ROWS, ROWS), 1)
    line = jnp.sum(jnp.where(on_diagonal, column, 0.0), 0, keepdims=True)
    sums_ref[...] = jnp.broadcast_to(line, (64, ROWS))


def before_kernel(
    second_ref,
    second_scale_ref,
    head_ref,
    out_weight_ref,
    proj_ref,
    probs_ref,
    select_ref,
    packed_ref,
    hidden_ref,
    attended_ref,
    scores_ref,
    back_ref,
    patch_w,
    sems,
):
    patch_copies = weight_copies(packed_ref, patch_w, sems, 0, 0, D)
    start_all(patch_copies)
    second = second_ref[...]
    direction = head_ref[0:1, :] / PATCHES
    hidden = norm_back(direction, second, second_scale_ref[:, 0:1])
    hidden_ref[...] = hidden
    grad_attended = dot_t(hidden.astype(BF16), out_weight_ref[...])
    attended_ref[...] = grad_attended
    low = half_mask()
    for pair in range(HEADS // 2):
        at = pair * 2 * HEAD_DIM
        value = proj_ref[:, 2 * INNER + at : 2 * INNER + at + 128]
        grad = grad_attended[:, at : at + 128]
        for side in range(2):
            mine = low if side == 0 else jnp.logical_not(low)
            grad_probs = dot_t(pick(mine, grad), value)
            probs = probs_ref[2 * pair + side]
            delta = jnp.sum(probs * grad_probs, -1, keepdims=True)
            scores_ref[2 * pair + side] = probs * (grad_probs - delta) * HEAD_DIM ** (-0.5)
    wait_all(patch_copies)
    back_ref[...] = dot(select_ref[...], patch_w[...].reshape(PADDED, D)).astype(BF16)


def backward_kernel(
    everyone_ref,
    scores_ref,
    attended_ref,
    hidden_ref,
    proj_ref,
    probs_ref,
    normed_ref,
    scale_ref,
    back_ref,
    packed_ref,
    grad_ref,
    rewards_ref,
    grad_proj,
    qkv_w,
    sems,
):
    qkv_copies = weight_copies(packed_ref, qkv_w, sems, 0, D, 3 * INNER)
    start_all(qkv_copies)
    total = jnp.sum(everyone_ref[...], 0, keepdims=True)
    same_frame = (iota((ROWS, ROWS), 0) & 63) == (iota((ROWS, ROWS), 1) & 63)
    rewards = jnp.sum(jnp.where(same_frame, total, 0.0), 1, keepdims=True) / PATCHES
    factor = -LOSS_SCALE / (1.0 + jnp.exp(rewards))
    on_diagonal = iota((ROWS, ROWS), 0) == iota((ROWS, ROWS), 1)
    line = jnp.sum(jnp.where(on_diagonal, rewards, 0.0), 0, keepdims=True)
    rewards_ref[...] = jnp.broadcast_to(line, (8, ROWS))
    low = half_mask()
    for pair in range(HEADS // 2):
        at = pair * 2 * HEAD_DIM
        query = proj_ref[:, at : at + 128]
        key = proj_ref[:, INNER + at : INNER + at + 128]
        grad = (factor * attended_ref[:, at : at + 128]).astype(BF16)
        parts = []
        for side in range(2):
            scores = (factor * scores_ref[2 * pair + side]).astype(BF16)
            probs = probs_ref[2 * pair + side].astype(BF16)
            parts.append((dot(scores, key), t_dot(scores, query), t_dot(probs, grad)))
        for part in range(3):
            grad_proj[:, part * INNER + at : part * INNER + at + 128] = jnp.where(
                low, parts[0][part], parts[1][part]
            ).astype(BF16)
    wait_all(qkv_copies)
    grad_first = dot_t(grad_proj[...], qkv_w[...].reshape(D, 3 * INNER))
    grad_embed = norm_back(grad_first, normed_ref[...], scale_ref[:, 0:1]).astype(BF16)
    grad_total = (factor * hidden_ref[...] + grad_embed.astype(F32)).astype(BF16)
    grad_ref[...] = dot_t(back_ref[...], grad_total).astype(BF16)


def conv_kernel(rows_ref, kernel_ref, out_ref):
    frames = rows_ref.shape[0]
    kernel = kernel_ref[...]
    lane = iota((16, IMAGE_W), 1)
    for frame in range(frames):
        rows = rows_ref[frame].astype(F32)
        right = jnp.where(lane == IMAGE_W - 1, 0.0, pltpu.roll(rows, IMAGE_W - 1, 1))
        left = jnp.where(lane == 0, 0.0, pltpu.roll(rows, 1, 1))
        taps = jnp.concatenate([right, rows, left], 0).astype(BF16)
        result = dot(kernel, taps).astype(BF16)
        for row in range(2):
            out_ref[frame, row] = result[row * 48 : (row + 1) * 48]


def shape(dims, dtype):
    return jax.ShapeDtypeStruct(dims, dtype)


def vmem(count):
    return [pl.BlockSpec(memory_space=pltpu.VMEM)] * count


ANYWHERE = pl.BlockSpec(memory_space=pl.ANY)
WEIGHT = (8, 4, 2, SLOT)


def to_patch_rows(pixels):
    frame_count, row_count, _, col_count = pixels.shape
    blocks = pixels.reshape(frame_count, row_count // PATCH, PATCH, 3, col_count // PATCH, PATCH)
    blocks = blocks.transpose(0, 1, 4, 3, 2, 5)
    return blocks.reshape(frame_count, row_count // PATCH * (col_count // PATCH), 3 * PATCH * PATCH)


def conv_matrix(conv_weight):
    flipped = conv_weight[::-1]
    per_row = jnp.stack(
        [jnp.pad(flipped, ((y, 1 - y), (0, 0), (0, 0), (0, 0))) for y in range(2)], 0
    )
    matrix = per_row.transpose(0, 3, 2, 1, 4).reshape(-1, 3, 12)
    return jnp.pad(matrix, ((0, 0), (0, 0), (0, 4))).reshape(-1, 48)


def gather_weights(patch_weight, qkv_weight, out_weight):
    half = out_weight.shape[1] // 2
    packed = jnp.concatenate(
        [
            jnp.pad(patch_weight, ((0, SLOT - patch_weight.shape[0]), (0, 0))),
            qkv_weight,
            jnp.concatenate([out_weight[:, :half], out_weight[:, half:]], 0),
        ],
        1,
    )
    return lax.all_gather(packed, "zh", axis=0)


def on_device(pixels, patch_weight, qkv_weight, out_weight, reward_head, conv_weight):
    near = gather_weights(patch_weight, qkv_weight, out_weight)
    near, pixels, conv_weight = lax.optimization_barrier((near, pixels, conv_weight))
    packed = lax.all_gather(near, ("y", "core"), axis=0)
    packed = packed.reshape(8, 2, 4, SLOT, packed.shape[-1])
    patches = to_patch_rows(pixels)
    spread = lax.all_to_all(patches, TILE, split_axis=1, concat_axis=0, tiled=True)
    spread, matrix = lax.optimization_barrier((spread, conv_matrix(conv_weight)))
    head = jnp.broadcast_to(reward_head[None], (8, D))
    slots, select = pl.pallas_call(
        spread_kernel,
        out_shape=(shape((ROWS, PADDED), BF16), shape((PDIM, PADDED), BF16)),
        name="spread",
    )(spread.reshape(ROWS, PDIM))
    normed, scale, proj, probs, second, second_scale, out_full, sums = pl.pallas_call(
        forward_kernel,
        out_shape=(
            shape((ROWS, D), F32),
            shape((ROWS, 128), F32),
            shape((ROWS, 3 * INNER), BF16),
            shape((HEADS, ROWS, ROWS), F32),
            shape((ROWS, D), F32),
            shape((ROWS, 128), F32),
            shape((INNER, D), BF16),
            shape((64, ROWS), F32),
        ),
        in_specs=vmem(1) + [ANYWHERE] + vmem(1),
        out_specs=tuple(vmem(8)),
        scratch_shapes=[
            pltpu.VMEM(WEIGHT + (D,), BF16),
            pltpu.VMEM(WEIGHT + (3 * INNER,), BF16),
            pltpu.VMEM(WEIGHT + (D // 2,), BF16),
            pltpu.SemaphoreType.DMA((24,)),
        ],
        name="forward",
    )(slots, packed, head)
    everyone = lax.all_to_all(sums, TILE, split_axis=0, concat_axis=0, tiled=True)
    hidden, attended, scores, back = pl.pallas_call(
        before_kernel,
        out_shape=(
            shape((ROWS, D), F32),
            shape((ROWS, INNER), F32),
            shape((HEADS, ROWS, ROWS), F32),
            shape((PDIM, D), BF16),
        ),
        in_specs=vmem(7) + [ANYWHERE],
        out_specs=tuple(vmem(4)),
        scratch_shapes=[pltpu.VMEM(WEIGHT + (D,), BF16), pltpu.SemaphoreType.DMA((8,))],
        cost_estimate=pl.CostEstimate(flops=2**31, transcendentals=0, bytes_accessed=2**23),
        name="before",
    )(second, second_scale, head, out_full, proj, probs, select, packed)
    grad, rewards = pl.pallas_call(
        backward_kernel,
        out_shape=(shape((PDIM, ROWS), BF16), shape((8, ROWS), F32)),
        in_specs=vmem(9) + [ANYWHERE],
        out_specs=tuple(vmem(2)),
        scratch_shapes=[
            pltpu.VMEM((ROWS, 3 * INNER), BF16),
            pltpu.VMEM(WEIGHT + (3 * INNER,), BF16),
            pltpu.SemaphoreType.DMA((8,)),
        ],
        name="backward",
    )(everyone, scores, attended, hidden, proj, probs, normed, scale, back, packed)
    row_grad = lax.all_to_all(
        grad.reshape(8, PDIM // 8, ROWS), ROW, split_axis=0, concat_axis=0, tiled=True
    )
    row_grad = row_grad.reshape(8, 2, 3 * PATCH, ROWS)
    devices = lax.axis_size(TILE)
    up = [(i, i + 1) for i in range(devices - 1)]
    down = [(i + 1, i) for i in range(devices - 1)]
    before = lax.ppermute(row_grad[:, 1], TILE, up)
    after = lax.ppermute(row_grad[:, 0], TILE, down)
    rows = jnp.concatenate([before[:, None], row_grad, after[:, None]], 1)
    rows = rows.reshape(8, 4, 3, PATCH, 2, FRAMES).transpose(5, 1, 2, 0, 4, 3)
    rows = jnp.pad(rows.reshape(FRAMES, 12, IMAGE_W), ((0, 0), (0, 4), (0, 0)))
    step = 8
    act_grad = pl.pallas_call(
        conv_kernel,
        out_shape=shape((FRAMES, 2, 48, IMAGE_W), BF16),
        grid=(FRAMES // step,),
        in_specs=[
            pl.BlockSpec((step, 16, IMAGE_W), lambda i: (i, 0, 0)),
            pl.BlockSpec((96, 48), lambda i: (0, 0)),
        ],
        out_specs=pl.BlockSpec((step, 2, 48, IMAGE_W), lambda i: (i, 0, 0, 0)),
        name="conv",
    )(rows, matrix)
    mine = lax.dynamic_slice_in_dim(rewards[0], lax.axis_index(TILE), 1)
    return (mine, act_grad)


def solution(mesh):
    axes = Mesh(mesh.devices.reshape(-1, 4, 8, 4, 2), GRP + TILE)
    in_specs = (
        P(GRP + TILE, None, None, None),
        P(TILE, None),
        P(TILE, None),
        P(TILE, None),
        P(),
        P(),
    )
    out_specs = (P(GRP + TILE), P(GRP, TILE, None, None))
    return jax.shard_map(
        on_device, mesh=axes, in_specs=in_specs, out_specs=out_specs, check_vma=False
    )
```

time: 224 us -> 165 us (0.74)
  waiting for transfers between devices: 84.8 us -> 37.6 us
  Pallas kernels: 0 us -> 31.3 us
  local copies, waits for them, and re-layouts: 35.7 us -> 13.2 us
  matrix products: 21.3 us -> 0 us
  starting transfers between devices: 13.6 us -> 31 us
  blocking collectives: 44.1 us -> 33 us
  other arithmetic: 8.83 us -> 3.99 us
    all_gather x1, waiting for transfers between devices: 66.4 us -> 12.8 us  [on_device(): packed = lax.all_gather(near, ('y', 'core'), axis=0)]
    all_to_all x2 -> x1, blocking collectives: 44.1 us -> 12.6 us  [on_device(): lax.all_to_all(grad.reshape(8, PDIM // 8, ROWS), ROW, split_axis=0, conca...]
    pallas_call x0 -> x5, Pallas kernels: none -> 31.3 us  [the longest x1 8.31 us: on_device(): pl.pallas_call(forward_kernel, out_shape=(shape((ROWS, D), F32), shape((R...]
    all_gather x0 -> x1, blocking collectives: none -> 20.3 us  [gather_weights(): return lax.all_gather(packed, 'zh', axis=0)]
    dot_general x12 -> x0, matrix products: 20 us -> none  [the longest x1 3.86 us: on_device(): jnp.einsum('fykx,kc->fycx', stacked, kernel, preferred_element_type=jnp.f...]
    all_to_all x1 -> x2, starting transfers between devices: 7.5 us -> 24.4 us  [the longest x1 13.7 us: on_device(): lax.all_to_all(patches, TILE, split_axis=1, concat_axis=0, tiled=True)]
    all_to_all x1 -> x2, waiting for transfers between devices: 10.8 us -> 21.2 us  [the longest x1 16.1 us: on_device(): lax.all_to_all(patches, TILE, split_axis=1, concat_axis=0, tiled=True)]
    another operation x5 -> x1, local copies, waits for them, and re-layouts: 6 us -> 0.01 us  [conv_matrix(): jnp.stack([jnp.pad(flipped, ((y, 1 - y), (0, 0), (0, 0), (0, 0))) for y i...]
  transfers between devices with their start and end apart: 4 -> 5, of which waited for: 4 -> 4; matrix products, arithmetic and copies ran while one was open for 3% -> 7% of each run, Pallas kernels for 0% -> 6%
where the time goes in v2:
time: 165 us; the launch traced here: 164 us
  waiting for transfers between devices  37.6 us (23%)
  blocking collectives  33 us (20%)
  Pallas kernels  31.3 us (19%)
  starting transfers between devices  31 us (19%)
  between operations  14.3 us (9%)
  local copies, waits for them, and re-layouts  13.2 us (8%)
  other arithmetic  3.99 us (2%)
    all_gather x1, blocking collectives, gather_weights(): return lax.all_gather(packed, 'zh', axis=0)  20.3 us
    all_to_all x1, waiting for transfers between devices, on_device(): lax.all_to_all(patches, TILE, split_axis=1, concat_axis=0, tiled=True)  16.1 us
    all_to_all x1, starting transfers between devices, on_device(): lax.all_to_all(patches, TILE, split_axis=1, concat_axis=0, tiled=True)  13.7 us
    all_gather x1, waiting for transfers between devices, on_device(): packed = lax.all_gather(near, ('y', 'core'), axis=0)  12.8 us
    all_to_all x1, blocking collectives, on_device(): lax.all_to_all(grad.reshape(8, PDIM // 8, ROWS), ROW, split_axis=0, conca...  12.6 us
    all_to_all x1, starting transfers between devices, on_device(): lax.all_to_all(sums, TILE, split_axis=0, concat_axis=0, tiled=True)  10.7 us
    pallas_call x1, Pallas kernels, on_device(): pl.pallas_call(forward_kernel, out_shape=(shape((ROWS, D), F32), shape((R...  8.31 us
    pallas_call x1, Pallas kernels, on_device(): pl.pallas_call(before_kernel, out_shape=(shape((ROWS, D), F32), shape((RO...  6.73 us
  transfers between devices with their start and end apart: 5, of which 4 were waited for; matrix products, arithmetic and copies ran while one was open for 7% of the time, Pallas kernels for 6%

profile of v2, /device:TPU:1, one launch (start us, length us, event | category | flops | bytes accessed | tf_op | source)
XLA Modules:
  0.0 164.4 jit_solution(13768411288144013789)
XLA Ops:
  7.2 0.7 fusion.3
  7.9 0.8 fusion.2
  8.8 20.3 %all-gather = bf16[64,3072]{1,0:T(8,128)(2,1)} all-gather(bf16[16,3072]{1,0:T(8,128)(2,1)S(1)} %fusion.2), channel_id=2, replica_groups=mesh['zl'=2,'x'=4,'y'=8,'zh'=4,'core'=2] {'zh'}, dimensions={0}, use_global_device_ids=true | all-gather | bytes 491520 | tf_op jit(solution)/shard_map/all_gather | solution.py:316
  29.1 2.1 %reshape.45 = bf16[1,8,16,3,16,16]{5,4,2,1,3,0:T(8,128)(2,1)S(1)} reshape(bf16[1,128,3,256]{3,1,2,0:T(8,128)(2,1)} %param.6) | data formatting | bytes 393216 | tf_op jit(solution)/shard_map/reshape | solution.py:292
  31.6 1.1 reshape.57
  32.7 0.5 broadcast.16
  33.2 1.8 %reduce.2 = bf16[128,768]{1,0:T(8,128)(2,1)S(1)} reduce(bf16[128,1,768]{2,1,0:T(2,128)(2,1)S(1)} %bitcast.46, bf16[]{:T(256)} %broadcast.16), dimensions={1}, to_apply=%bitcast.35.reduce_sub_computation | reduce | bytes 393218
  35.1 0.8 reshape.59
  35.8 13.7 %all-to-all-start = ((bf16[64,2,768]{2,1,0:T(2,128)(2,1)}), bf16[64,2,768]{2,1,0:T(2,128)(2,1)S(1)}, u32[]{:S(2)}, u32[]{:S(2)}) async-start(bf16[64,2,768]{2,1,0:T(2,128)(2,1)} %reshape.59), calls=%async_computation | async-start | bytes 393216 | tf_op jit(solution)/shard_map/all_to_all | solution.py:325
  49.7 16.1 %all-to-all-done = bf16[64,2,768]{2,1,0:T(2,128)(2,1)S(1)} async-done(((bf16[64,2,768]{2,1,0:T(2,128)(2,1)}), bf16[64,2,768]{2,1,0:T(2,128)(2,1)S(1)}, u32[]{:S(2)}, u32[]{:S(2)}) %all-to-all-start) | async-done | bytes 196640 | tf_op jit(solution)/shard_map/all_to_all | solution.py:325
  66.0 1.1 bitcast_reduce_fusion
  67.2 0.8 reshape.49.patches_ref
  68.0 3.2 %spread.1 = (bf16[128,1024]{1,0:T(8,128)(2,1)}, bf16[768,1024]{1,0:T(8,128)(2,1)}) custom-call(bf16[128,768]{1,0:T(8,128)(2,1)} %reshape.49.patches_ref), custom_call_target="tpu_custom_call" | custom-call | tf_op jit(solution)/shard_map/spread/pallas_call | solution.py:328
  71.2 12.8 %all-gather.4.cloned.1.call-done = bf16[64,16,3072]{2,1,0:T(8,128)(2,1)} async-done(((bf16[4,16,3072]{2,1,0:T(8,128)(2,1)}), bf16[64,16,3072]{2,1,0:T(8,128)(2,1)}) %all-gather.4.cloned.1.call-update) | async-done | bytes 6291472 | tf_op jit(solution)/shard_map/all_gather | solution.py:322
  84.0 0.6 broadcast_in_dim.2.head_ref
  84.6 8.3 %forward.1 = (f32[128,1024]{1,0:T(8,128)}, f32[128,128]{1,0:T(8,128)}, bf16[128,1536]{1,0:T(8,128)(2,1)}, f32[8,128,128]{2,1,0:T(8,128)}, f32[128,1024]{1,0:T(8,...) custom-call(bf16[128,1024]{1,0:T(8,128)(2,1)} %get-tuple-element.26.patches_ref, ...), custom_call_target="tpu_custom_call" | custom-call | tf_op jit(solution)/shard_map/forward/pallas_call | solution.py:333
  92.9 10.7 %all-to-all-start.1 = ((f32[64,1,128]{2,1,0:T(1,128)}), f32[64,1,128]{2,1,0:T(1,128)S(1)}, u32[]{:S(2)}, u32[]{:S(2)}) async-start(f32[64,1,128]{2,1,0:T(1,128)} %bitcast.52), calls=%async_computation.1 | async-start | bytes 65536 | tf_op jit(solution)/shard_map/all_to_all | solution.py:355
  103.6 6.7 %before.1 = (f32[128,1024]{1,0:T(8,128)}, f32[128,512]{1,0:T(8,128)}, f32[8,128,128]{2,1,0:T(8,128)}, bf16[768,1024]{1,0:T(8,128)(2,1)}) custom-call(f32[128,1024]{1,0:T(8,128)} %get-tuple-element.29.second_ref, f32[128,128]{1,0:T(8,128)} %get-tuple-element.30.second_scale_ref, f32[8,1024]{1,0:T(8,128)} %broadcast_in_dim.2.head_ref, ...), custom_call_target="tpu_custom_call" | custom-call | flops 2147483648 | bytes 8388608 | tf_op jit(solution)/shard_map/before/pallas_call | solution.py:356
  110.4 5.0 %all-to-all-done.1 = f32[64,1,128]{2,1,0:T(1,128)S(1)} async-done(((f32[64,1,128]{2,1,0:T(1,128)}), f32[64,1,128]{2,1,0:T(1,128)S(1)}, u32[]{:S(2)}, u32[]{:S(2)}) %all-to-all-start.1) | async-done | bytes 32800 | tf_op jit(solution)/shard_map/all_to_all | solution.py:355
  115.4 0.6 copy-done
  116.0 6.7 %backward.1 = (bf16[768,128]{1,0:T(8,128)(2,1)}, f32[8,128]{1,0:T(8,128)}) custom-call(f32[64,128]{1,0:T(8,128)} %bitcast.50, f32[8,128,128]{2,1,0:T(8,128)} %get-tuple-element.35.scores_ref, f32[128,512]{1,0:T(8,128)} %get-tuple-element.36.attended_ref, f32[128,1024]{1,0:T(8,128)} %get-tuple-element.37.hidden_ref, ...), custom_call_target="tpu_custom_call" | custom-call | tf_op jit(solution)/shard_map/backward/pallas_call | solution.py:370
  122.8 12.6 %all_to_all.28 = bf16[8,96,128]{2,1,0:T(8,128)(2,1)S(1)} all-to-all(bf16[8,96,128]{2,1,0:T(8,128)(2,1)} %bitcast.49), channel_id=1, replica_groups=mesh['zl'=2,'x'=4,'y'=8,'zh'=4,'core'=2] {'zh','core'}, dimensions={0} | all-to-all | bytes 393216 | tf_op jit(solution)/shard_map/all_to_all | solution.py:382
  135.4 4.6 %collective-permute-start = (bf16[8,48,128]{2,1,0:T(8,128)(2,1)S(1)}, bf16[8,48,128]{2,1,0:T(8,128)(2,1)S(1)}, u32[]{:S(2)}, u32[]{:S(2)}) collective-permute-start(bf16[8,48,128]{2,1,0:T(8,128)(2,1)S(1)} %get-tuple-element.44), channel_id=1, source_target_pairs={{0,1},{1,2},{2,3},{3,4},{4,5},{5,6},{6,7},{7,8},{8,9},{9,10},{10,1... | collective-permute-start | bytes 294920 | tf_op jit(solution)/shard_map/ppermute | solution.py:389
  140.0 1.9 %collective-permute-start.1 = (bf16[8,48,128]{2,1,0:T(8,128)(2,1)S(1)}, bf16[8,48,128]{2,1,0:T(8,128)(2,1)S(1)}, u32[]{:S(2)}, u32[]{:S(2)}) collective-permute-start(bf16[8,48,128]{2,1,0:T(8,128)(2,1)S(1)} %get-tuple-element.45), channel_id=1, source_target_pairs={{1,0},{2,1},{3,2},{4,3},{5,4},{6,5},{7,6},{8,7},{9,8},{10,9},{11,1... | collective-permute-start | bytes 294920 | tf_op jit(solution)/shard_map/ppermute | solution.py:390
  142.0 0.7 copy.39.kernel_ref
  142.7 0.7 slice.17
  143.4 0.6 constant_dynamic-slice_fusion
  144.3 3.6 %collective-permute-done.1 = bf16[8,48,128]{2,1,0:T(8,128)(2,1)S(1)} collective-permute-done((bf16[8,48,128]{2,1,0:T(8,128)(2,1)S(1)}, bf16[8,48,128]{2,1,0:T(8,128)(2,1)S(1)}, u32[]{:S(2)}, u32[]{:S(2)}) %collective-permute-start.1) | collective-permute-done | bytes 98336 | tf_op jit(solution)/shard_map/ppermute | solution.py:390
  148.0 1.3 maximum_bitcast_fusion
  149.5 0.8 copy.38
  150.3 0.9 pad.24.rows_ref
  151.2 6.4 %conv.1 = bf16[64,2,48,256]{3,2,1,0:T(8,128)(2,1)} custom-call(bf16[64,16,256]{2,1,0:T(8,128)(2,1)} %pad.24.rows_ref, bf16[96,48]{1,0:T(8,128)(2,1)} %copy.39.kernel_ref), custom_call_target="tpu_custom_call" | custom-call | tf_op jit(solution)/shard_map/conv/pallas_call | solution.py:395
  (22 shorter events, 1.4 us)
Async XLA Ops:
  7.2 76.8 %all-gather.4.cloned.1.call-start = ((), (), s32[]{:S(2)}) async-start(), calls=%async_computation.3 | async-start | bytes 6684672 | tf_op jit(solution)/shard_map/all_gather | solution.py:322
  31.6 17.9 %copy-start.1 = (bf16[3,3,48,3]{2,3,1,0:T(4,128)(2,1)S(1)}, bf16[3,3,48,3]{2,3,1,0:T(4,128)(2,1)}, u32[]{:S(2)}) copy-start(bf16[3,3,48,3]{2,3,1,0:T(4,128)(2,1)} %param.11) | copy-start | bytes 7780
  35.0 48.9 %copy-start.2 = (f32[1024]{0:T(1024)S(1)}, f32[1024]{0:T(1024)}, u32[]{:S(2)}) copy-start(f32[1024]{0:T(1024)} %param.10) | copy-start | bytes 12292
  35.8 30.0 %all-to-all-start = ((bf16[64,2,768]{2,1,0:T(2,128)(2,1)}), bf16[64,2,768]{2,1,0:T(2,128)(2,1)S(1)}, u32[]{:S(2)}, u32[]{:S(2)}) async-start(bf16[64,2,768]{2,1,0:T(2,128)(2,1)} %reshape.59), calls=%async_computation | async-start | bytes 393216 | tf_op jit(solution)/shard_map/all_to_all | solution.py:325
  92.9 22.5 %all-to-all-start.1 = ((f32[64,1,128]{2,1,0:T(1,128)}), f32[64,1,128]{2,1,0:T(1,128)S(1)}, u32[]{:S(2)}, u32[]{:S(2)}) async-start(f32[64,1,128]{2,1,0:T(1,128)} %bitcast.52), calls=%async_computation.1 | async-start | bytes 65536 | tf_op jit(solution)/shard_map/all_to_all | solution.py:355
  115.4 0.6 copy-start
  135.4 8.7 %collective-permute-start = (bf16[8,48,128]{2,1,0:T(8,128)(2,1)S(1)}, bf16[8,48,128]{2,1,0:T(8,128)(2,1)S(1)}, u32[]{:S(2)}, u32[]{:S(2)}) collective-permute-start(bf16[8,48,128]{2,1,0:T(8,128)(2,1)S(1)} %get-tuple-element.44), channel_id=1, source_target_pairs={{0,1},{1,2},{2,3},{3,4},{4,5},{5,6},{6,7},{7,8},{8,9},{9,10},{10,1... | collective-permute-start | bytes 294920 | tf_op jit(solution)/shard_map/ppermute | solution.py:389
  140.0 7.8 %collective-permute-start.1 = (bf16[8,48,128]{2,1,0:T(8,128)(2,1)S(1)}, bf16[8,48,128]{2,1,0:T(8,128)(2,1)S(1)}, u32[]{:S(2)}, u32[]{:S(2)}) collective-permute-start(bf16[8,48,128]{2,1,0:T(8,128)(2,1)S(1)} %get-tuple-element.45), channel_id=1, source_target_pairs={{1,0},{2,1},{3,2},{4,3},{5,4},{6,5},{7,6},{8,7},{9,8},{10,9},{11,1... | collective-permute-start | bytes 294920 | tf_op jit(solution)/shard_map/ppermute | solution.py:390
Sparse Core Ops, SparseCore 0:
  29.2 54.7 all-gather.3

commit v3 on v2

v3 whole, which is shorter than its diff:
```python
import jax
import jax.numpy as jnp
from jax import lax
from jax.experimental import pallas as pl
from jax.experimental.pallas import tpu as pltpu
from jax.sharding import Mesh
from jax.sharding import PartitionSpec as P

D = 1024
HEADS = 8
HEAD_DIM = 64
PATCH = 16
PDIM = 768
INNER = HEADS * HEAD_DIM
SLOT = 16
SHARE = 12
PATCH_AT, QKV_AT, TAIL_AT, OUT_AT, BLOCK = 0, 48, 112, 144, 176
FRAMES = 64
PATCHES = 128
ROWS = 128
IMAGE_W = 256
TOGETHER = 4
MIB = 2**20

GRP = ("zl", "x")
TILE = ("y", "zh", "core")
ROW = ("zh", "core")

LOSS_SCALE = 1024.0
NORM_EPSILON = 1e-05
F32 = jnp.float32
BF16 = jnp.bfloat16


def iota(shape, dim):
    return lax.broadcasted_iota(jnp.int32, shape, dim)


def dot(a, b):
    return lax.dot_general(a, b, (((1,), (0,)), ((), ())), preferred_element_type=F32)


def dot_t(a, b):
    return lax.dot_general(a, b, (((1,), (1,)), ((), ())), preferred_element_type=F32)


def one_hot(condition):
    return jnp.where(condition, 1.0, 0.0).astype(F32).astype(BF16)


def normalize(values_in):
    centred = values_in - jnp.mean(values_in, -1, keepdims=True)
    inverse_scale = lax.rsqrt(jnp.mean(centred * centred, -1, keepdims=True) + NORM_EPSILON)
    return centred * inverse_scale, inverse_scale


def norm_back(grad_in, normed, inverse_scale):
    return inverse_scale * (
        grad_in
        - jnp.mean(grad_in, -1, keepdims=True)
        - normed * jnp.mean(grad_in * normed, -1, keepdims=True)
    )


def weight_copies(packed, sems, moves):
    copies = []
    for row, rows, column, columns, target in moves:
        for part in range(4):
            copies.append(
                pltpu.make_async_copy(
                    packed.at[4 * part : 4 * part + 4, row : row + rows, column : column + columns],
                    target(slice(4 * part, 4 * part + 4)),
                    sems.at[len(copies)],
                )
            )
    return copies


def qkv_moves(target, low, high):
    head, tail = D - low, high - D
    return [
        (QKV_AT, 64, low, head, lambda part: target.at[part, :, 0:head]),
        (TAIL_AT, 32, 0, tail, lambda part: target.at[part, 0:32, head : head + tail]),
        (TAIL_AT, 32, tail, tail, lambda part: target.at[part, 32:64, head : head + tail]),
    ]


def start_all(copies):
    for copy in copies:
        copy.start()


def wait_all(copies):
    for copy in copies:
        copy.wait()


def arrange_kernel(core_ref, near_ref, out_ref):
    slots = near_ref[pl.ds(4 * core_ref[0], 4)].reshape(4 * SLOT, 3 * D)
    slot = iota((48, 4 * SLOT), 1)
    row = jnp.where((slot & 15) < SHARE, SHARE * (slot >> 4) + (slot & 15), -1)
    take = one_hot(row == iota((48, 4 * SLOT), 0))
    out_ref[PATCH_AT:QKV_AT] = dot(take, slots[:, 0:D]).astype(BF16)
    out_ref[QKV_AT:TAIL_AT] = slots[:, D : 2 * D]
    out_ref[TAIL_AT:OUT_AT, 0:INNER] = slots[0:32, 2 * D : 2 * D + INNER]
    out_ref[TAIL_AT:OUT_AT, INNER:D] = slots[32:64, 2 * D : 2 * D + INNER]
    slot = iota((32, 4 * SLOT), 1)
    for half in range(2):
        row = jnp.where(((slot >> 3) & 1) == half, 8 * (slot >> 4) + (slot & 7), -1)
        take = one_hot(row == iota((32, 4 * SLOT), 0))
        out_ref[OUT_AT:BLOCK, half * INNER : (half + 1) * INNER] = dot(
            take, slots[:, 2 * D + INNER : 3 * D]
        ).astype(BF16)


def spread_kernel(patches_ref, out_ref):
    to_row = iota((ROWS, ROWS), 0)
    order = one_hot(iota((ROWS, ROWS), 1) == 2 * (to_row & (FRAMES - 1)) + (to_row >> 6))
    out_ref[...] = dot(order, patches_ref[...]).astype(BF16)


def half_mask():
    return iota((ROWS, 2 * HEAD_DIM), 1) < HEAD_DIM


def pick(condition, value):
    return jnp.where(condition, value.astype(F32), 0.0).astype(BF16)


def forward_kernel(
    patches_ref,
    packed_ref,
    head_ref,
    normed_out,
    scale_out,
    proj_out,
    probs_out,
    second_out,
    second_scale_out,
    sums_ref,
    patch_w,
    qkv_w,
    out_w,
    normed_ref,
    scale_ref,
    proj_ref,
    probs_ref,
    second_ref,
    second_scale_ref,
    patch_sems,
    qkv_sems,
    weight_sems,
    out_sems,
):
    results = [
        pltpu.make_async_copy(source, target, out_sems.at[i])
        for i, (source, target) in enumerate(
            [
                (normed_ref, normed_out),
                (scale_ref, scale_out),
                (proj_ref, proj_out),
                (second_ref, second_out),
                (second_scale_ref, second_scale_out),
            ]
            + [(probs_ref.at[2 * i : 2 * i + 2], probs_out.at[2 * i : 2 * i + 2]) for i in range(4)]
        )
    ]
    patch_copies = weight_copies(
        packed_ref, patch_sems, [(PATCH_AT, 48, 0, D, lambda part: patch_w.at[part])]
    )
    qkv_copies = weight_copies(packed_ref, qkv_sems, qkv_moves(qkv_w, 0, 3 * INNER))
    out_copies = weight_copies(
        packed_ref, weight_sems, [(OUT_AT, 32, 0, D, lambda part: out_w.at[part])]
    )
    start_all(patch_copies + qkv_copies + out_copies)
    wait_all(patch_copies)
    embedded = dot(patches_ref[...], patch_w[...].reshape(PDIM, D)).astype(BF16).astype(F32)
    normed, scale = normalize(embedded)
    normed_ref[...] = normed
    scale_ref[...] = jnp.broadcast_to(scale, (ROWS, 128))
    start_all(results[0:2])
    wait_all(qkv_copies)
    proj_ref[...] = dot(normed.astype(BF16), qkv_w[...].reshape(D, 3 * INNER)).astype(BF16)
    start_all(results[2:3])
    same_patch = (iota((ROWS, ROWS), 0) >> 6) == (iota((ROWS, ROWS), 1) >> 6)
    low = half_mask()
    attended = []
    for pair in range(HEADS // 2):
        at = pair * 2 * HEAD_DIM
        query = proj_ref[:, at : at + 128]
        key = proj_ref[:, INNER + at : INNER + at + 128]
        value = proj_ref[:, 2 * INNER + at : 2 * INNER + at + 128]
        parts = []
        for side in range(2):
            mine = low if side == 0 else jnp.logical_not(low)
            scores = dot_t(pick(mine, query), key) * HEAD_DIM ** (-0.5)
            scores = jnp.where(same_patch, scores, -1e30)
            weights = jnp.exp(scores - jnp.max(scores, -1, keepdims=True))
            probs = weights / jnp.sum(weights, -1, keepdims=True)
            probs_ref[2 * pair + side] = probs
            parts.append(dot(probs.astype(BF16), value))
        results[5 + pair].start()
        attended.append(jnp.where(low, parts[0], parts[1]).astype(BF16))
    wait_all(out_copies)
    hidden = embedded + dot(jnp.concatenate(attended, 1), out_w[...].reshape(INNER, D))
    second, second_scale = normalize(hidden)
    second_ref[...] = second
    second_scale_ref[...] = jnp.broadcast_to(second_scale, (ROWS, 128))
    start_all(results[3:5])
    column = jnp.sum(second * head_ref[0:1, :], -1, keepdims=True)
    on_diagonal = iota((ROWS, ROWS), 0) == iota((ROWS, ROWS), 1)
    line = jnp.sum(jnp.where(on_diagonal, column, 0.0), 0, keepdims=True)
    sums_ref[...] = jnp.broadcast_to(line, (64, ROWS))
    wait_all(results)


def before_kernel(
    second_ref,
    second_scale_ref,
    head_ref,
    proj_ref,
    probs_ref,
    packed_ref,
    hidden_ref,
    attended_ref,
    scores_ref,
    probs_t_ref,
    query_part_ref,
    out_w,
    query_w,
    out_sems,
    query_sems,
):
    out_copies = weight_copies(
        packed_ref, out_sems, [(OUT_AT, 32, 0, D, lambda part: out_w.at[part])]
    )
    query_copies = weight_copies(
        packed_ref, query_sems, [(QKV_AT, 64, 0, INNER, lambda part: query_w.at[part])]
    )
    start_all(out_copies + query_copies)
    second = second_ref[...]
    direction = head_ref[0:1, :] / PATCHES
    hidden = norm_back(direction, second, second_scale_ref[:, 0:1])
    hidden_ref[...] = hidden
    wait_all(out_copies)
    grad_attended = dot_t(hidden.astype(BF16), out_w[...].reshape(INNER, D))
    attended_ref[...] = grad_attended
    low = half_mask()
    grad_query = []
    for pair in range(HEADS // 2):
        at = pair * 2 * HEAD_DIM
        key = proj_ref[:, INNER + at : INNER + at + 128]
        value = proj_ref[:, 2 * INNER + at : 2 * INNER + at + 128]
        grad = grad_attended[:, at : at + 128]
        parts = []
        for side in range(2):
            mine = low if side == 0 else jnp.logical_not(low)
            grad_probs = dot_t(pick(mine, grad), value)
            probs = probs_ref[2 * pair + side]
            delta = jnp.sum(probs * grad_probs, -1, keepdims=True)
            scores = probs * (grad_probs - delta) * HEAD_DIM ** (-0.5)
            parts.append(dot(scores.astype(BF16), key))
            scores_ref[2 * pair + side] = scores.T
            probs_t_ref[2 * pair + side] = probs.T.astype(BF16)
        grad_query.append(jnp.where(low, parts[0], parts[1]).astype(BF16))
    wait_all(query_copies)
    query_part_ref[...] = dot_t(jnp.concatenate(grad_query, 1), query_w[...].reshape(D, INNER))


def backward_kernel(
    everyone_ref,
    scores_in,
    attended_in,
    hidden_in,
    proj_in,
    probs_t_in,
    query_part_in,
    normed_in,
    scale_in,
    packed_ref,
    grad_ref,
    rewards_ref,
    scores_ref,
    attended_ref,
    hidden_ref,
    proj_ref,
    probs_t_ref,
    query_part_ref,
    normed_ref,
    scale_ref,
    grad_proj,
    rest_w,
    patch_w,
    rest_sems,
    patch_sems,
    in_sems,
):
    arrivals = [
        pltpu.make_async_copy(source, target, in_sems.at[i])
        for i, (source, target) in enumerate(
            [
                (scores_in, scores_ref),
                (proj_in.at[:, 0:INNER], proj_ref),
                (probs_t_in, probs_t_ref),
                (attended_in, attended_ref),
                (query_part_in, query_part_ref),
                (normed_in, normed_ref),
                (scale_in, scale_ref),
                (hidden_in, hidden_ref),
            ]
        )
    ]
    rest_copies = weight_copies(packed_ref, rest_sems, qkv_moves(rest_w, INNER, 3 * INNER))
    patch_copies = weight_copies(
        packed_ref, patch_sems, [(PATCH_AT, 48, 0, D, lambda part: patch_w.at[part])]
    )
    start_all(arrivals[0:4] + rest_copies + arrivals[4:] + patch_copies)
    total = jnp.sum(everyone_ref[...], 0, keepdims=True)
    same_frame = (iota((ROWS, ROWS), 0) & 63) == (iota((ROWS, ROWS), 1) & 63)
    rewards = jnp.sum(jnp.where(same_frame, total, 0.0), 1, keepdims=True) / PATCHES
    on_diagonal = iota((ROWS, ROWS), 0) == iota((ROWS, ROWS), 1)
    line = jnp.sum(jnp.where(on_diagonal, rewards, 0.0), 0, keepdims=True)
    factor = -LOSS_SCALE / (1.0 + jnp.exp(rewards))
    factor_line = -LOSS_SCALE / (1.0 + jnp.exp(line))
    rewards_ref[...] = jnp.broadcast_to(line, (8, ROWS))
    low = half_mask()
    wait_all(arrivals[0:4])
    for pair in range(HEADS // 2):
        at = pair * 2 * HEAD_DIM
        query = proj_ref[:, at : at + 128]
        grad = (factor * attended_ref[:, at : at + 128]).astype(BF16)
        parts = []
        for side in range(2):
            scores = (factor_line * scores_ref[2 * pair + side]).astype(BF16)
            parts.append((dot(scores, query), dot(probs_t_ref[2 * pair + side], grad)))
        for part in range(2):
            grad_proj[:, part * INNER + at : part * INNER + at + 128] = jnp.where(
                low, parts[0][part], parts[1][part]
            ).astype(BF16)
    wait_all(rest_copies + arrivals[4:])
    grad_first = factor * query_part_ref[...] + dot_t(
        grad_proj[...], rest_w[...].reshape(D, 2 * INNER)
    )
    grad_embed = norm_back(grad_first, normed_ref[...], scale_ref[:, 0:1]).astype(BF16)
    grad_total = (factor * hidden_ref[...] + grad_embed.astype(F32)).astype(BF16)
    wait_all(patch_copies)
    grad = dot_t(patch_w[...].reshape(PDIM, D), grad_total).astype(BF16)
    for block in range(PDIM // PATCH):
        colour, row = block // PATCH, block % PATCH
        at = ((row // 2) * 6 + (row % 2) * 3 + colour) * PATCH
        grad_ref[at : at + PATCH] = grad[block * PATCH : (block + 1) * PATCH]


def conv_kernel(rows_ref, kernel_ref, out_ref):
    kernel = kernel_ref[...]
    lane = iota((16, IMAGE_W), 1)
    for first in range(0, rows_ref.shape[0], TOGETHER):
        taps = []
        for frame in range(first, first + TOGETHER):
            rows = rows_ref[frame].astype(F32)
            right = jnp.where(lane == IMAGE_W - 1, 0.0, pltpu.roll(rows, IMAGE_W - 1, 1))
            left = jnp.where(lane == 0, 0.0, pltpu.roll(rows, 1, 1))
            taps += [right.astype(BF16), rows_ref[frame], left.astype(BF16)]
        result = dot(kernel, jnp.concatenate(taps, 0)).astype(BF16)
        for frame in range(TOGETHER):
            for row in range(2):
                at = (frame * 2 + row) * 48
                out_ref[first + frame, row] = result[at : at + 48]


def shape(dims, dtype):
    return jax.ShapeDtypeStruct(dims, dtype)


def vmem(count):
    return [pl.BlockSpec(memory_space=pltpu.VMEM)] * count


ANYWHERE = pl.BlockSpec(memory_space=pl.ANY)


def to_patch_rows(pixels):
    frame_count, row_count, _, col_count = pixels.shape
    blocks = pixels.reshape(frame_count, row_count // PATCH, PATCH, 3, col_count // PATCH, PATCH)
    blocks = blocks.transpose(0, 1, 4, 3, 2, 5)
    return blocks.reshape(frame_count, row_count // PATCH * (col_count // PATCH), 3 * PATCH * PATCH)


def conv_matrix(conv_weight):
    flipped = conv_weight[::-1]
    per_row = jnp.stack(
        [jnp.pad(flipped, ((y, 1 - y), (0, 0), (0, 0), (0, 0))) for y in range(2)], 0
    )
    per_row = jnp.pad(per_row, ((0, 0), (0, 0), (0, 0), (0, 0), (0, 1)))
    matrix = per_row.transpose(0, 3, 2, 1, 4).reshape(-1, 48)
    zero = jnp.zeros_like(matrix)
    return jnp.concatenate(
        [
            jnp.concatenate([matrix if i == j else zero for j in range(TOGETHER)], 1)
            for i in range(TOGETHER)
        ],
        0,
    )


def gather_weights(patch_weight, qkv_weight, out_weight):
    half = out_weight.shape[1] // 2
    packed = jnp.concatenate(
        [
            jnp.pad(patch_weight, ((0, SLOT - patch_weight.shape[0]), (0, 0))),
            qkv_weight,
            jnp.concatenate([out_weight[:, :half], out_weight[:, half:]], 0),
        ],
        1,
    )
    near = lax.all_gather(packed, ROW, axis=0)
    core = lax.axis_index("core").astype(jnp.int32).reshape(1)
    return pl.pallas_call(
        arrange_kernel,
        out_shape=shape((BLOCK, D), BF16),
        in_specs=[pl.BlockSpec(memory_space=pltpu.SMEM)] + vmem(1),
        out_specs=vmem(1)[0],
        compiler_params=pltpu.CompilerParams(vmem_limit_bytes=8 * MIB),
        name="arrange",
    )(core, near)


def on_device(pixels, patch_weight, qkv_weight, out_weight, reward_head, conv_weight):
    near = gather_weights(patch_weight, qkv_weight, out_weight)
    near, pixels, conv_weight = lax.optimization_barrier((near, pixels, conv_weight))
    packed = lax.all_gather(near, ("y", "core"), axis=0)
    patches = to_patch_rows(pixels)
    spread = lax.all_to_all(patches, TILE, split_axis=1, concat_axis=0, tiled=True)
    head = jnp.broadcast_to(reward_head[None], (8, D))
    spread, matrix, head = lax.optimization_barrier((spread, conv_matrix(conv_weight), head))
    ordered = pl.pallas_call(
        spread_kernel,
        out_shape=shape((ROWS, PDIM), BF16),
        compiler_params=pltpu.CompilerParams(vmem_limit_bytes=8 * MIB),
        name="spread",
    )(spread.reshape(ROWS, PDIM))
    normed, scale, proj, probs, second, second_scale, sums = pl.pallas_call(
        forward_kernel,
        out_shape=(
            shape((ROWS, D), F32),
            shape((ROWS, 128), F32),
            shape((ROWS, 3 * INNER), BF16),
            shape((HEADS, ROWS, ROWS), F32),
            shape((ROWS, D), F32),
            shape((ROWS, 128), F32),
            shape((64, ROWS), F32),
        ),
        in_specs=vmem(1) + [ANYWHERE] + vmem(1),
        out_specs=tuple([ANYWHERE] * 6 + vmem(1)),
        scratch_shapes=[
            pltpu.VMEM((16, 48, D), BF16),
            pltpu.VMEM((16, 64, 3 * INNER), BF16),
            pltpu.VMEM((16, 32, D), BF16),
            pltpu.VMEM((ROWS, D), F32),
            pltpu.VMEM((ROWS, 128), F32),
            pltpu.VMEM((ROWS, 3 * INNER), BF16),
            pltpu.VMEM((HEADS, ROWS, ROWS), F32),
            pltpu.VMEM((ROWS, D), F32),
            pltpu.VMEM((ROWS, 128), F32),
            pltpu.SemaphoreType.DMA((4,)),
            pltpu.SemaphoreType.DMA((12,)),
            pltpu.SemaphoreType.DMA((4,)),
            pltpu.SemaphoreType.DMA((9,)),
        ],
        name="forward",
    )(ordered, packed, head)
    everyone = lax.all_to_all(sums, TILE, split_axis=0, concat_axis=0, tiled=True)
    hidden, attended, scores, probs_t, query_part = pl.pallas_call(
        before_kernel,
        out_shape=(
            shape((ROWS, D), F32),
            shape((ROWS, INNER), F32),
            shape((HEADS, ROWS, ROWS), F32),
            shape((HEADS, ROWS, ROWS), BF16),
            shape((ROWS, D), F32),
        ),
        in_specs=vmem(5) + [ANYWHERE],
        out_specs=tuple(vmem(5)),
        scratch_shapes=[
            pltpu.VMEM((16, 32, D), BF16),
            pltpu.VMEM((16, 64, INNER), BF16),
            pltpu.SemaphoreType.DMA((4,)),
            pltpu.SemaphoreType.DMA((4,)),
        ],
        cost_estimate=pl.CostEstimate(flops=2**30, transcendentals=0, bytes_accessed=2**23),
        name="before",
    )(second, second_scale, head, proj, probs, packed)
    grad, rewards = pl.pallas_call(
        backward_kernel,
        out_shape=(shape((PDIM, ROWS), BF16), shape((8, ROWS), F32)),
        in_specs=vmem(1) + [ANYWHERE] * 9,
        out_specs=tuple(vmem(2)),
        scratch_shapes=[
            pltpu.VMEM((HEADS, ROWS, ROWS), F32),
            pltpu.VMEM((ROWS, INNER), F32),
            pltpu.VMEM((ROWS, D), F32),
            pltpu.VMEM((ROWS, INNER), BF16),
            pltpu.VMEM((HEADS, ROWS, ROWS), BF16),
            pltpu.VMEM((ROWS, D), F32),
            pltpu.VMEM((ROWS, D), F32),
            pltpu.VMEM((ROWS, 128), F32),
            pltpu.VMEM((ROWS, 2 * INNER), BF16),
            pltpu.VMEM((16, 64, 2 * INNER), BF16),
            pltpu.VMEM((16, 48, D), BF16),
            pltpu.SemaphoreType.DMA((12,)),
            pltpu.SemaphoreType.DMA((4,)),
            pltpu.SemaphoreType.DMA((8,)),
        ],
        name="backward",
    )(
        everyone, scores, attended, hidden, proj, probs_t, query_part, normed, scale, packed
    )
    row_grad = lax.all_to_all(
        grad.reshape(8, PDIM // 8, ROWS), ROW, split_axis=0, concat_axis=0, tiled=True
    )
    row_grad = row_grad.reshape(8, 2, 3 * PATCH, ROWS)
    devices = lax.axis_size(TILE)
    up = [(i, i + 1) for i in range(devices - 1)]
    down = [(i + 1, i) for i in range(devices - 1)]
    before = lax.ppermute(row_grad[:, 1], TILE, up)
    after = lax.ppermute(row_grad[:, 0], TILE, down)
    rows = jnp.concatenate([before[:, None], row_grad, after[:, None]], 1)
    rows = jnp.pad(rows, ((0, 0), (0, 0), (0, PATCH), (0, 0)))
    rows = rows.reshape(8, 4, 4, PATCH, 2, FRAMES).transpose(5, 1, 2, 0, 4, 3)
    rows = rows.reshape(FRAMES, 16, IMAGE_W)
    step = 16
    act_grad = pl.pallas_call(
        conv_kernel,
        out_shape=shape((FRAMES, 2, 48, IMAGE_W), BF16),
        grid=(FRAMES // step,),
        in_specs=[
            pl.BlockSpec((step, 16, IMAGE_W), lambda i: (i, 0, 0)),
            pl.BlockSpec((96 * TOGETHER, 48 * TOGETHER), lambda i: (0, 0)),
        ],
        out_specs=pl.BlockSpec((step, 2, 48, IMAGE_W), lambda i: (i, 0, 0, 0)),
        compiler_params=pltpu.CompilerParams(vmem_limit_bytes=8 * MIB),
        name="conv",
    )(rows, matrix)
    mine = lax.dynamic_slice_in_dim(rewards[0], lax.axis_index(TILE), 1)
    return (mine, act_grad)


def solution(mesh):
    axes = Mesh(mesh.devices.reshape(-1, 4, 8, 4, 2), GRP + TILE)
    in_specs = (
        P(GRP + TILE, None, None, None),
        P(TILE, None),
        P(TILE, None),
        P(TILE, None),
        P(),
        P(),
    )
    out_specs = (P(GRP + TILE), P(GRP, TILE, None, None))
    return jax.shard_map(
        on_device, mesh=axes, in_specs=in_specs, out_specs=out_specs, check_vma=False
    )
```

time: 165 us -> 158 us (0.958)
  Pallas kernels: 31.3 us -> 24.7 us
  starting transfers between devices: 31 us -> 28.6 us
  blocking collectives: 33 us -> 35.2 us
  waiting for transfers between devices: 37.6 us -> 39.6 us
    pallas_call x1, Pallas kernels: 6.37 us -> 3.13 us  [on_device(): pl.pallas_call(conv_kernel, out_shape=shape((FRAMES, 2, 48, IMAGE_W), BF1...]
    all_gather x1, blocking collectives: 20.3 us -> 22.6 us  [gather_weights(): near = lax.all_gather(packed, ROW, axis=0)]
    all_to_all x1, starting transfers between devices: 13.7 us -> 11.4 us  [on_device(): lax.all_to_all(patches, TILE, split_axis=1, concat_axis=0, tiled=True)]
    pallas_call x1 -> x2, Pallas kernels: 3.21 us -> 1.11 us  [the longest x1 0.92 us: gather_weights(): pl.pallas_call(arrange_kernel, out_shape=shape((BLOCK, D), BF16), in_spec...]
  transfers between devices with their start and end apart: 5 -> 5, of which waited for: 4 -> 4; matrix products, arithmetic and copies ran while one was open for 7% -> 7% of each run, Pallas kernels for 6% -> 4%
where the time goes in v3:
time: 158 us; the launch traced here: 157 us
  waiting for transfers between devices  39.6 us (25%)
  blocking collectives  35.2 us (22%)
  starting transfers between devices  28.6 us (18%)
  Pallas kernels  24.7 us (16%)
  between operations  14.3 us (9%)
  local copies, waits for them, and re-layouts  11.9 us (8%)
  other arithmetic  2.84 us (2%)
    all_gather x1, blocking collectives, gather_weights(): near = lax.all_gather(packed, ROW, axis=0)  22.6 us
    all_to_all x1, waiting for transfers between devices, on_device(): lax.all_to_all(patches, TILE, split_axis=1, concat_axis=0, tiled=True)  15.8 us
    all_gather x1, waiting for transfers between devices, on_device(): packed = lax.all_gather(near, ('y', 'core'), axis=0)  13.5 us
    all_to_all x1, blocking collectives, on_device(): lax.all_to_all(grad.reshape(8, PDIM // 8, ROWS), ROW, split_axis=0, conca...  12.6 us
    all_to_all x1, starting transfers between devices, on_device(): lax.all_to_all(patches, TILE, split_axis=1, concat_axis=0, tiled=True)  11.4 us
    all_to_all x1, starting transfers between devices, on_device(): lax.all_to_all(sums, TILE, split_axis=0, concat_axis=0, tiled=True)  10.5 us
    pallas_call x1, Pallas kernels, on_device(): pl.pallas_call(forward_kernel, out_shape=(shape((ROWS, D), F32), shape((R...  8.3 us
    pallas_call x1, Pallas kernels, on_device(): pl.pallas_call(before_kernel, out_shape=(shape((ROWS, D), F32), shape((RO...  6.15 us
  transfers between devices with their start and end apart: 5, of which 4 were waited for; matrix products, arithmetic and copies ran while one was open for 7% of the time, Pallas kernels for 4%

profile of v3, /device:TPU:1, one launch (start us, length us, event | category | flops | bytes accessed | tf_op | source)
XLA Modules:
  0.0 157.1 jit_solution(4743639555947105228)
XLA Ops:
  7.2 0.7 fusion.17
  7.9 0.8 fusion.12
  8.8 22.6 %all-gather = bf16[128,3072]{1,0:T(8,128)(2,1)S(1)} all-gather(bf16[16,3072]{1,0:T(8,128)(2,1)S(1)} %fusion.12), channel_id=2, replica_groups=mesh['zl'=2,'x'=4,'y'=8,'zh'=4,'core'=2] {'zh','core'}, dimensions={0}, use_global_device_ids=true | all-gather | bytes 884736 | tf_op jit(solution)/shard_map/all_gather | solution.py:416
  31.3 0.9 arrange.1
  32.3 2.1 %reshape.39 = bf16[1,8,16,3,16,16]{5,4,2,1,3,0:T(8,128)(2,1)S(1)} reshape(bf16[1,128,3,256]{3,1,2,0:T(8,128)(2,1)} %param.6) | data formatting | bytes 393216 | tf_op jit(solution)/shard_map/reshape | solution.py:384
  34.4 0.4 copy.59
  34.8 1.1 reshape.49
  35.9 0.5 broadcast.46
  36.4 1.8 %reduce.2 = bf16[128,768]{1,0:T(8,128)(2,1)S(1)} reduce(bf16[128,1,768]{2,1,0:T(2,128)(2,1)S(1)} %bitcast.53, bf16[]{:T(256)} %broadcast.46), dimensions={1}, to_apply=%bitcast.40.reduce_sub_computation | reduce | bytes 393218
  38.2 0.8 reshape.51
  39.0 11.4 %all-to-all-start = ((bf16[64,2,768]{2,1,0:T(2,128)(2,1)}), bf16[64,2,768]{2,1,0:T(2,128)(2,1)S(1)}, u32[]{:S(2)}, u32[]{:S(2)}) async-start(bf16[64,2,768]{2,1,0:T(2,128)(2,1)} %reshape.51), calls=%async_computation | async-start | bytes 393216 | tf_op jit(solution)/shard_map/all_to_all | solution.py:433
  50.9 15.8 %all-to-all-done = bf16[64,2,768]{2,1,0:T(2,128)(2,1)S(1)} async-done(((bf16[64,2,768]{2,1,0:T(2,128)(2,1)}), bf16[64,2,768]{2,1,0:T(2,128)(2,1)S(1)}, u32[]{:S(2)}, u32[]{:S(2)}) %all-to-all-start) | async-done | bytes 196640 | tf_op jit(solution)/shard_map/all_to_all | solution.py:433
  66.9 1.1 bitcast_reduce_fusion
  68.1 0.6 broadcast_in_dim.16.head_ref
  69.0 0.7 copy-done
  69.7 13.5 %all-gather.4.cloned.1.call-done = bf16[2816,1024]{1,0:T(8,128)(2,1)} async-done(((bf16[176,1024]{1,0:T(8,128)(2,1)}), bf16[2816,1024]{1,0:T(8,128)(2,1)}) %all-gather.4.cloned.1.call-update) | async-done | bytes 5767184 | tf_op jit(solution)/shard_map/all_gather | solution.py:431
  83.1 8.3 %forward.1 = (f32[128,1024]{1,0:T(8,128)}, f32[128,128]{1,0:T(8,128)}, bf16[128,1536]{1,0:T(8,128)(2,1)}, f32[8,128,128]{2,1,0:T(8,128)}, f32[128,1024]{1,0:T(8,...) custom-call(bf16[128,768]{1,0:T(8,128)(2,1)} %copy-done, bf16[16,176,1024]{2,1,0:T(8,128)(2,1)} %bitcast.45, ...), custom_call_target="tpu_custom_call" | custom-call | tf_op jit(solution)/shard_map/forward/pallas_call | solution.py:442
  91.5 10.5 %all-to-all-start.1 = ((f32[64,1,128]{2,1,0:T(1,128)}), f32[64,1,128]{2,1,0:T(1,128)S(1)}, u32[]{:S(2)}, u32[]{:S(2)}) async-start(f32[64,1,128]{2,1,0:T(1,128)} %bitcast.58), calls=%async_computation.1 | async-start | bytes 65536 | tf_op jit(solution)/shard_map/all_to_all | solution.py:472
  102.0 6.2 %before.1 = (f32[128,1024]{1,0:T(8,128)}, f32[128,512]{1,0:T(8,128)}, f32[8,128,128]{2,1,0:T(8,128)}, bf16[8,128,128]{2,1,0:T(8,128)(2,1)}, f32[128,1024]{1,0:T(8,128)}) custom-call(f32[128,1024]{1,0:T(8,128)} %get-tuple-element.28.second_ref, f32[128,128]{1,0:T(8,128)} %get-tuple-element.29.second_scale_ref, f32[8,1024]{1,0:T(8,128)} %broadcast_in_dim.16.head_ref, ...), custom_call_target="tpu_custom_call" | custom-call | flops 1073741824 | bytes 8388608 | tf_op jit(solution)/shard_map/before/pallas_call | solution.py:473
  108.1 5.6 %all-to-all-done.1 = f32[64,1,128]{2,1,0:T(1,128)S(1)} async-done(((f32[64,1,128]{2,1,0:T(1,128)}), f32[64,1,128]{2,1,0:T(1,128)S(1)}, u32[]{:S(2)}, u32[]{:S(2)}) %all-to-all-start.1) | async-done | bytes 32800 | tf_op jit(solution)/shard_map/all_to_all | solution.py:472
  113.8 0.6 copy-done.1
  114.4 6.0 %backward.1 = (bf16[768,128]{1,0:T(8,128)(2,1)}, f32[8,128]{1,0:T(8,128)}) custom-call(f32[64,128]{1,0:T(8,128)} %bitcast.55, f32[8,128,128]{2,1,0:T(8,128)} %get-tuple-element.32.scores_in, f32[128,512]{1,0:T(8,128)} %get-tuple-element.33.attended_in, f32[128,1024]{1,0:T(8,128)} %get-tuple-element.34.hidden_in, ...), custom_call_target="tpu_custom_call" | custom-call | tf_op jit(solution)/shard_map/backward/pallas_call | solution.py:493
  120.4 12.6 %all_to_all.28 = bf16[8,96,128]{2,1,0:T(8,128)(2,1)S(1)} all-to-all(bf16[8,96,128]{2,1,0:T(8,128)(2,1)} %bitcast.54), channel_id=1, replica_groups=mesh['zl'=2,'x'=4,'y'=8,'zh'=4,'core'=2] {'zh','core'}, dimensions={0} | all-to-all | bytes 393216 | tf_op jit(solution)/shard_map/all_to_all | solution.py:518
  133.0 4.7 %collective-permute-start = (bf16[8,48,128]{2,1,0:T(8,128)(2,1)S(1)}, bf16[8,48,128]{2,1,0:T(8,128)(2,1)S(1)}, u32[]{:S(2)}, u32[]{:S(2)}) collective-permute-start(bf16[8,48,128]{2,1,0:T(8,128)(2,1)S(1)} %get-tuple-element.42), channel_id=1, source_target_pairs={{0,1},{1,2},{2,3},{3,4},{4,5},{5,6},{6,7},{7,8},{8,9},{9,10},{10,1... | collective-permute-start | bytes 294920 | tf_op jit(solution)/shard_map/ppermute | solution.py:525
  137.7 1.9 %collective-permute-start.1 = (bf16[8,48,128]{2,1,0:T(8,128)(2,1)S(1)}, bf16[8,48,128]{2,1,0:T(8,128)(2,1)S(1)}, u32[]{:S(2)}, u32[]{:S(2)}) collective-permute-start(bf16[8,48,128]{2,1,0:T(8,128)(2,1)S(1)} %get-tuple-element.43), channel_id=1, source_target_pairs={{1,0},{2,1},{3,2},{4,3},{5,4},{6,5},{7,6},{8,7},{9,8},{10,9},{11,1... | collective-permute-start | bytes 294920 | tf_op jit(solution)/shard_map/ppermute | solution.py:526
  139.7 0.7 slice.17
  140.3 0.6 constant_dynamic-slice_fusion
  140.9 4.6 %collective-permute-done.1 = bf16[8,48,128]{2,1,0:T(8,128)(2,1)S(1)} collective-permute-done((bf16[8,48,128]{2,1,0:T(8,128)(2,1)S(1)}, bf16[8,48,128]{2,1,0:T(8,128)(2,1)S(1)}, u32[]{:S(2)}, u32[]{:S(2)}) %collective-permute-start.1) | collective-permute-done | bytes 98336 | tf_op jit(solution)/shard_map/ppermute | solution.py:526
  145.6 0.4 reshape.45
  146.0 0.2 copy.53
  146.3 0.8 copy.54.rows_ref
  147.1 3.1 %conv.1 = bf16[64,2,48,256]{3,2,1,0:T(8,128)(2,1)} custom-call(bf16[64,16,256]{2,1,0:T(8,128)(2,1)S(1)} %copy.54.rows_ref, bf16[384,192]{1,0:T(8,128)(2,1)S(1)} %fusion.7.kernel_ref), custom_call_target="tpu_custom_call" | custom-call | tf_op jit(solution)/shard_map/conv/pallas_call | solution.py:532
  (24 shorter events, 1.0 us)
Async XLA Ops:
  7.2 76.0 %all-gather.4.cloned.1.call-start = ((), (), s32[]{:S(2)}) async-start(), calls=%async_computation.3 | async-start | bytes 6127616 | tf_op jit(solution)/shard_map/all_gather | solution.py:431
  34.4 16.1 %copy-start.2 = (bf16[3,3,48,3]{2,3,1,0:T(4,128)(2,1)S(1)}, bf16[3,3,48,3]{2,3,1,0:T(4,128)(2,1)}, u32[]{:S(2)}) copy-start(bf16[3,3,48,3]{2,3,1,0:T(4,128)(2,1)} %param.11) | copy-start | bytes 7780
  34.8 33.3 %copy-start.3 = (f32[1024]{0:T(1024)S(1)}, f32[1024]{0:T(1024)}, u32[]{:S(2)}) copy-start(f32[1024]{0:T(1024)} %param.10) | copy-start | bytes 12292
  39.0 27.7 %all-to-all-start = ((bf16[64,2,768]{2,1,0:T(2,128)(2,1)}), bf16[64,2,768]{2,1,0:T(2,128)(2,1)S(1)}, u32[]{:S(2)}, u32[]{:S(2)}) async-start(bf16[64,2,768]{2,1,0:T(2,128)(2,1)} %reshape.51), calls=%async_computation | async-start | bytes 393216 | tf_op jit(solution)/shard_map/all_to_all | solution.py:433
  69.0 0.7 copy-start
  91.5 22.3 %all-to-all-start.1 = ((f32[64,1,128]{2,1,0:T(1,128)}), f32[64,1,128]{2,1,0:T(1,128)S(1)}, u32[]{:S(2)}, u32[]{:S(2)}) async-start(f32[64,1,128]{2,1,0:T(1,128)} %bitcast.58), calls=%async_computation.1 | async-start | bytes 65536 | tf_op jit(solution)/shard_map/all_to_all | solution.py:472
  113.8 0.6 copy-start.1
  133.0 7.9 %collective-permute-start = (bf16[8,48,128]{2,1,0:T(8,128)(2,1)S(1)}, bf16[8,48,128]{2,1,0:T(8,128)(2,1)S(1)}, u32[]{:S(2)}, u32[]{:S(2)}) collective-permute-start(bf16[8,48,128]{2,1,0:T(8,128)(2,1)S(1)} %get-tuple-element.42), channel_id=1, source_target_pairs={{0,1},{1,2},{2,3},{3,4},{4,5},{5,6},{6,7},{7,8},{8,9},{9,10},{10,1... | collective-permute-start | bytes 294920 | tf_op jit(solution)/shard_map/ppermute | solution.py:525
  137.7 7.8 %collective-permute-start.1 = (bf16[8,48,128]{2,1,0:T(8,128)(2,1)S(1)}, bf16[8,48,128]{2,1,0:T(8,128)(2,1)S(1)}, u32[]{:S(2)}, u32[]{:S(2)}) collective-permute-start(bf16[8,48,128]{2,1,0:T(8,128)(2,1)S(1)} %get-tuple-element.43), channel_id=1, source_target_pairs={{1,0},{2,1},{3,2},{4,3},{5,4},{6,5},{7,6},{8,7},{9,8},{10,9},{11,1... | collective-permute-start | bytes 294920 | tf_op jit(solution)/shard_map/ppermute | solution.py:526
Sparse Core Ops, SparseCore 0:
  32.4 50.6 all-gather.3

commit v4 on v3

--- a/solution.py
+++ b/solution.py
@@ -21,6 +21,7 @@
 IMAGE_W = 256
 TOGETHER = 4
 MIB = 2**20
+CHUNKS = 4
 
 GRP = ("zl", "x")
 TILE = ("y", "zh", "core")
@@ -65,11 +66,12 @@
 def weight_copies(packed, sems, moves):
     copies = []
     for row, rows, column, columns, target in moves:
-        for part in range(4):
+        for part in range(CHUNKS):
+            mine = slice(part * 16 // CHUNKS, (part + 1) * 16 // CHUNKS)
             copies.append(
                 pltpu.make_async_copy(
-                    packed.at[4 * part : 4 * part + 4, row : row + rows, column : column + columns],
-                    target(slice(4 * part, 4 * part + 4)),
+                    packed.at[mine, row : row + rows, column : column + columns],
+                    target(mine),
                     sems.at[len(copies)],
                 )
             )
@@ -137,7 +139,7 @@
     probs_out,
     second_out,
     second_scale_out,
-    sums_ref,
+    sums_out,
     patch_w,
     qkv_w,
     out_w,
@@ -147,6 +149,7 @@
     probs_ref,
     second_ref,
     second_scale_ref,
+    sums_ref,
     patch_sems,
     qkv_sems,
     weight_sems,
@@ -163,6 +166,7 @@
                 (second_scale_ref, second_scale_out),
             ]
             + [(probs_ref.at[2 * i : 2 * i + 2], probs_out.at[2 * i : 2 * i + 2]) for i in range(4)]
+            + [(sums_ref, sums_out)]
         )
     ]
     patch_copies = weight_copies(
@@ -211,16 +215,25 @@
     on_diagonal = iota((ROWS, ROWS), 0) == iota((ROWS, ROWS), 1)
     line = jnp.sum(jnp.where(on_diagonal, column, 0.0), 0, keepdims=True)
     sums_ref[...] = jnp.broadcast_to(line, (64, ROWS))
+    start_all(results[9:])
     wait_all(results)
 
 
 def before_kernel(
-    second_ref,
+    second_in,
     second_scale_ref,
     head_ref,
+    proj_in,
+    probs_in,
+    packed_ref,
+    hidden_out,
+    attended_out,
+    scores_out,
+    probs_t_out,
+    query_part_out,
+    second_ref,
     proj_ref,
     probs_ref,
-    packed_ref,
     hidden_ref,
     attended_ref,
     scores_ref,
@@ -230,21 +243,46 @@
     query_w,
     out_sems,
     query_sems,
+    in_sems,
+    result_sems,
 ):
+    arrivals = [
+        pltpu.make_async_copy(source, target, in_sems.at[i])
+        for i, (source, target) in enumerate(
+            [(second_in, second_ref), (proj_in, proj_ref), (probs_in, probs_ref)]
+        )
+    ]
+    results = [
+        pltpu.make_async_copy(source, target, result_sems.at[i])
+        for i, (source, target) in enumerate(
+            [
+                (hidden_ref, hidden_out),
+                (attended_ref, attended_out),
+                (scores_ref, scores_out),
+                (probs_t_ref, probs_t_out),
+                (query_part_ref, query_part_out),
+            ]
+        )
+    ]
     out_copies = weight_copies(
         packed_ref, out_sems, [(OUT_AT, 32, 0, D, lambda part: out_w.at[part])]
     )
     query_copies = weight_copies(
         packed_ref, query_sems, [(QKV_AT, 64, 0, INNER, lambda part: query_w.at[part])]
     )
+    start_all(arrivals)
     start_all(out_copies + query_copies)
+    arrivals[0].wait()
     second = second_ref[...]
     direction = head_ref[0:1, :] / PATCHES
     hidden = norm_back(direction, second, second_scale_ref[:, 0:1])
     hidden_ref[...] = hidden
+    results[0].start()
     wait_all(out_copies)
     grad_attended = dot_t(hidden.astype(BF16), out_w[...].reshape(INNER, D))
     attended_ref[...] = grad_attended
+    results[1].start()
+    wait_all(arrivals[1:])
     low = half_mask()
     grad_query = []
     for pair in range(HEADS // 2):
@@ -263,12 +301,16 @@
             scores_ref[2 * pair + side] = scores.T
             probs_t_ref[2 * pair + side] = probs.T.astype(BF16)
         grad_query.append(jnp.where(low, parts[0], parts[1]).astype(BF16))
+    start_all(results[2:4])
     wait_all(query_copies)
     query_part_ref[...] = dot_t(jnp.concatenate(grad_query, 1), query_w[...].reshape(D, INNER))
+    results[4].start()
+    wait_all(results)
 
 
 def backward_kernel(
-    everyone_ref,
+    tile_ref,
+    everyone_in,
     scores_in,
     attended_in,
     hidden_in,
@@ -294,6 +336,7 @@
     rest_sems,
     patch_sems,
     in_sems,
+    everyone_ref,
 ):
     arrivals = [
         pltpu.make_async_copy(source, target, in_sems.at[i])
@@ -307,6 +350,7 @@
                 (normed_in, normed_ref),
                 (scale_in, scale_ref),
                 (hidden_in, hidden_ref),
+                (everyone_in, everyone_ref),
             ]
         )
     ]
@@ -314,7 +358,8 @@
     patch_copies = weight_copies(
         packed_ref, patch_sems, [(PATCH_AT, 48, 0, D, lambda part: patch_w.at[part])]
     )
-    start_all(arrivals[0:4] + rest_copies + arrivals[4:] + patch_copies)
+    start_all(arrivals[8:] + arrivals[0:4] + rest_copies + arrivals[4:8] + patch_copies)
+    arrivals[8].wait()
     total = jnp.sum(everyone_ref[...], 0, keepdims=True)
     same_frame = (iota((ROWS, ROWS), 0) & 63) == (iota((ROWS, ROWS), 1) & 63)
     rewards = jnp.sum(jnp.where(same_frame, total, 0.0), 1, keepdims=True) / PATCHES
@@ -322,7 +367,7 @@
     line = jnp.sum(jnp.where(on_diagonal, rewards, 0.0), 0, keepdims=True)
     factor = -LOSS_SCALE / (1.0 + jnp.exp(rewards))
     factor_line = -LOSS_SCALE / (1.0 + jnp.exp(line))
-    rewards_ref[...] = jnp.broadcast_to(line, (8, ROWS))
+    rewards_ref[0] = jnp.sum(jnp.where(iota((1, ROWS), 1) == tile_ref[0], line, 0.0))
     low = half_mask()
     wait_all(arrivals[0:4])
     for pair in range(HEADS // 2):
@@ -337,7 +382,7 @@
             grad_proj[:, part * INNER + at : part * INNER + at + 128] = jnp.where(
                 low, parts[0][part], parts[1][part]
             ).astype(BF16)
-    wait_all(rest_copies + arrivals[4:])
+    wait_all(rest_copies + arrivals[4:8])
     grad_first = factor * query_part_ref[...] + dot_t(
         grad_proj[...], rest_w[...].reshape(D, 2 * INNER)
     )
@@ -351,16 +396,16 @@
         grad_ref[at : at + PATCH] = grad[block * PATCH : (block + 1) * PATCH]
 
 
-def conv_kernel(rows_ref, kernel_ref, out_ref):
+def conv_kernel(own_ref, halo_ref, kernel_ref, out_ref):
     kernel = kernel_ref[...]
     lane = iota((16, IMAGE_W), 1)
-    for first in range(0, rows_ref.shape[0], TOGETHER):
+    for first in range(0, own_ref.shape[0], TOGETHER):
         taps = []
         for frame in range(first, first + TOGETHER):
-            rows = rows_ref[frame].astype(F32)
+            rows = jnp.concatenate([own_ref[frame].astype(F32), halo_ref[frame].astype(F32)], 0)
             right = jnp.where(lane == IMAGE_W - 1, 0.0, pltpu.roll(rows, IMAGE_W - 1, 1))
             left = jnp.where(lane == 0, 0.0, pltpu.roll(rows, 1, 1))
-            taps += [right.astype(BF16), rows_ref[frame], left.astype(BF16)]
+            taps += [right.astype(BF16), rows.astype(BF16), left.astype(BF16)]
         result = dot(kernel, jnp.concatenate(taps, 0)).astype(BF16)
         for frame in range(TOGETHER):
             for row in range(2):
@@ -377,6 +422,7 @@
 
 
 ANYWHERE = pl.BlockSpec(memory_space=pl.ANY)
+SCALARS = pl.BlockSpec(memory_space=pltpu.SMEM)
 
 
 def to_patch_rows(pixels):
@@ -392,6 +438,7 @@
         [jnp.pad(flipped, ((y, 1 - y), (0, 0), (0, 0), (0, 0))) for y in range(2)], 0
     )
     per_row = jnp.pad(per_row, ((0, 0), (0, 0), (0, 0), (0, 0), (0, 1)))
+    per_row = jnp.concatenate([per_row[:, 1:3], per_row[:, 0:1], per_row[:, 3:4]], 1)
     matrix = per_row.transpose(0, 3, 2, 1, 4).reshape(-1, 48)
     zero = jnp.zeros_like(matrix)
     return jnp.concatenate(
@@ -401,6 +448,12 @@
         ],
         0,
     )
+
+
+def image_rows(received):
+    padded = jnp.pad(received, ((0, 0), (0, 0), (0, PATCH), (0, 0)))
+    rows = padded.reshape(8, 2, 4, PATCH, 2, FRAMES).transpose(5, 1, 2, 0, 4, 3)
+    return rows.reshape(FRAMES, 8, IMAGE_W)
 
 
 def gather_weights(patch_weight, qkv_weight, out_weight):
@@ -418,7 +471,7 @@
     return pl.pallas_call(
         arrange_kernel,
         out_shape=shape((BLOCK, D), BF16),
-        in_specs=[pl.BlockSpec(memory_space=pltpu.SMEM)] + vmem(1),
+        in_specs=[SCALARS] + vmem(1),
         out_specs=vmem(1)[0],
         compiler_params=pltpu.CompilerParams(vmem_limit_bytes=8 * MIB),
         name="arrange",
@@ -451,7 +504,7 @@
             shape((64, ROWS), F32),
         ),
         in_specs=vmem(1) + [ANYWHERE] + vmem(1),
-        out_specs=tuple([ANYWHERE] * 6 + vmem(1)),
+        out_specs=tuple([ANYWHERE] * 7),
         scratch_shapes=[
             pltpu.VMEM((16, 48, D), BF16),
             pltpu.VMEM((16, 64, 3 * INNER), BF16),
@@ -462,10 +515,11 @@
             pltpu.VMEM((HEADS, ROWS, ROWS), F32),
             pltpu.VMEM((ROWS, D), F32),
             pltpu.VMEM((ROWS, 128), F32),
-            pltpu.SemaphoreType.DMA((4,)),
-            pltpu.SemaphoreType.DMA((12,)),
-            pltpu.SemaphoreType.DMA((4,)),
-            pltpu.SemaphoreType.DMA((9,)),
+            pltpu.VMEM((64, ROWS), F32),
+            pltpu.SemaphoreType.DMA((CHUNKS,)),
+            pltpu.SemaphoreType.DMA((3 * CHUNKS,)),
+            pltpu.SemaphoreType.DMA((CHUNKS,)),
+            pltpu.SemaphoreType.DMA((10,)),
         ],
         name="forward",
     )(ordered, packed, head)
@@ -479,22 +533,33 @@
             shape((HEADS, ROWS, ROWS), BF16),
             shape((ROWS, D), F32),
         ),
-        in_specs=vmem(5) + [ANYWHERE],
-        out_specs=tuple(vmem(5)),
+        in_specs=[ANYWHERE] + vmem(2) + [ANYWHERE] * 3,
+        out_specs=tuple([ANYWHERE] * 5),
         scratch_shapes=[
+            pltpu.VMEM((ROWS, D), F32),
+            pltpu.VMEM((ROWS, 3 * INNER), BF16),
+            pltpu.VMEM((HEADS, ROWS, ROWS), F32),
+            pltpu.VMEM((ROWS, D), F32),
+            pltpu.VMEM((ROWS, INNER), F32),
+            pltpu.VMEM((HEADS, ROWS, ROWS), F32),
+            pltpu.VMEM((HEADS, ROWS, ROWS), BF16),
+            pltpu.VMEM((ROWS, D), F32),
             pltpu.VMEM((16, 32, D), BF16),
             pltpu.VMEM((16, 64, INNER), BF16),
-            pltpu.SemaphoreType.DMA((4,)),
-            pltpu.SemaphoreType.DMA((4,)),
+            pltpu.SemaphoreType.DMA((CHUNKS,)),
+            pltpu.SemaphoreType.DMA((CHUNKS,)),
+            pltpu.SemaphoreType.DMA((3,)),
+            pltpu.SemaphoreType.DMA((5,)),
         ],
         cost_estimate=pl.CostEstimate(flops=2**30, transcendentals=0, bytes_accessed=2**23),
         name="before",
     )(second, second_scale, head, proj, probs, packed)
+    tile = lax.axis_index(TILE).astype(jnp.int32).reshape(1)
     grad, rewards = pl.pallas_call(
         backward_kernel,
-        out_shape=(shape((PDIM, ROWS), BF16), shape((8, ROWS), F32)),
-        in_specs=vmem(1) + [ANYWHERE] * 9,
-        out_specs=tuple(vmem(2)),
+        out_shape=(shape((PDIM, ROWS), BF16), shape((1,), F32)),
+        in_specs=[SCALARS] + [ANYWHERE] * 10,
+        out_specs=(vmem(1)[0], SCALARS),
         scratch_shapes=[
             pltpu.VMEM((HEADS, ROWS, ROWS), F32),
             pltpu.VMEM((ROWS, INNER), F32),
@@ -507,13 +572,14 @@
             pltpu.VMEM((ROWS, 2 * INNER), BF16),
             pltpu.VMEM((16, 64, 2 * INNER), BF16),
             pltpu.VMEM((16, 48, D), BF16),
-            pltpu.SemaphoreType.DMA((12,)),
-            pltpu.SemaphoreType.DMA((4,)),
-            pltpu.SemaphoreType.DMA((8,)),
+            pltpu.SemaphoreType.DMA((3 * CHUNKS,)),
+            pltpu.SemaphoreType.DMA((CHUNKS,)),
+            pltpu.SemaphoreType.DMA((9,)),
+            pltpu.VMEM((64, ROWS), F32),
         ],
         name="backward",
     )(
-        everyone, scores, attended, hidden, proj, probs_t, query_part, normed, scale, packed
+        tile, everyone, scores, attended, hidden, proj, probs_t, query_part, normed, scale, packed
     )
     row_grad = lax.all_to_all(
         grad.reshape(8, PDIM // 8, ROWS), ROW, split_axis=0, concat_axis=0, tiled=True
@@ -524,25 +590,23 @@
     down = [(i + 1, i) for i in range(devices - 1)]
     before = lax.ppermute(row_grad[:, 1], TILE, up)
     after = lax.ppermute(row_grad[:, 0], TILE, down)
-    rows = jnp.concatenate([before[:, None], row_grad, after[:, None]], 1)
-    rows = jnp.pad(rows, ((0, 0), (0, 0), (0, PATCH), (0, 0)))
-    rows = rows.reshape(8, 4, 4, PATCH, 2, FRAMES).transpose(5, 1, 2, 0, 4, 3)
-    rows = rows.reshape(FRAMES, 16, IMAGE_W)
+    own = image_rows(row_grad)
+    halo = image_rows(jnp.stack([before, after], 1))
     step = 16
     act_grad = pl.pallas_call(
         conv_kernel,
         out_shape=shape((FRAMES, 2, 48, IMAGE_W), BF16),
         grid=(FRAMES // step,),
         in_specs=[
-            pl.BlockSpec((step, 16, IMAGE_W), lambda i: (i, 0, 0)),
+            pl.BlockSpec((step, 8, IMAGE_W), lambda i: (i, 0, 0)),
+            pl.BlockSpec((step, 8, IMAGE_W), lambda i: (i, 0, 0)),
             pl.BlockSpec((96 * TOGETHER, 48 * TOGETHER), lambda i: (0, 0)),
         ],
         out_specs=pl.BlockSpec((step, 2, 48, IMAGE_W), lambda i: (i, 0, 0, 0)),
         compiler_params=pltpu.CompilerParams(vmem_limit_bytes=8 * MIB),
         name="conv",
-    )(rows, matrix)
-    mine = lax.dynamic_slice_in_dim(rewards[0], lax.axis_index(TILE), 1)
-    return (mine, act_grad)
+    )(own, halo, matrix)
+    return (rewards, act_grad)
 
 
 def solution(mesh):

time: 158 us -> 155 us (0.981)
  transfers between devices with their start and end apart: 5 -> 5, of which waited for: 4 -> 4; matrix products, arithmetic and copies ran while one was open for 7% -> 6% of each run, Pallas kernels for 4% -> 4%
where the time goes in v4:
time: 155 us
  waiting for transfers between devices  40.1 us (26%)
  blocking collectives  35.2 us (23%)
  starting transfers between devices  28.6 us (18%)
  Pallas kernels  23.4 us (15%)
  between operations  14.4 us (9%)
  local copies, waits for them, and re-layouts  10.5 us (7%)
  other arithmetic  2.79 us (2%)
    all_gather x1, blocking collectives, gather_weights(): near = lax.all_gather(packed, ROW, axis=0)  22.6 us
    all_to_all x1, waiting for transfers between devices, on_device(): lax.all_to_all(patches, TILE, split_axis=1, concat_axis=0, tiled=True)  15.7 us
    all_gather x1, waiting for transfers between devices, on_device(): packed = lax.all_gather(near, ('y', 'core'), axis=0)  13.5 us
    all_to_all x1, blocking collectives, on_device(): lax.all_to_all(grad.reshape(8, PDIM // 8, ROWS), ROW, split_axis=0, conca...  12.6 us
    all_to_all x1, starting transfers between devices, on_device(): lax.all_to_all(patches, TILE, split_axis=1, concat_axis=0, tiled=True)  11.4 us
    all_to_all x1, starting transfers between devices, on_device(): lax.all_to_all(sums, TILE, split_axis=0, concat_axis=0, tiled=True)  10.5 us
    pallas_call x1, Pallas kernels, on_device(): pl.pallas_call(forward_kernel, out_shape=(shape((ROWS, D), F32), shape((R...  7.72 us
    pallas_call x1, Pallas kernels, on_device(): pl.pallas_call(before_kernel, out_shape=(shape((ROWS, D), F32), shape((RO...  6.16 us
  transfers between devices with their start and end apart: 5, of which 4 were waited for; matrix products, arithmetic and copies ran while one was open for 6% of the time, Pallas kernels for 4%

profile of v4, /device:TPU:1, one launch (start us, length us, event | category | flops | bytes accessed | tf_op | source)
XLA Modules:
  0.0 154.9 jit_solution(8316422974592480031)
XLA Ops:
  7.2 0.7 fusion.12
  7.9 0.8 fusion.7
  8.8 22.6 %all-gather = bf16[128,3072]{1,0:T(8,128)(2,1)S(1)} all-gather(bf16[16,3072]{1,0:T(8,128)(2,1)S(1)} %fusion.7), channel_id=2, replica_groups=mesh['zl'=2,'x'=4,'y'=8,'zh'=4,'core'=2] {'zh','core'}, dimensions={0}, use_global_device_ids=true | all-gather | bytes 884736 | tf_op jit(solution)/shard_map/all_gather | solution.py:469
  31.3 0.9 arrange.1
  32.3 2.1 %reshape.48 = bf16[1,8,16,3,16,16]{5,4,2,1,3,0:T(8,128)(2,1)S(1)} reshape(bf16[1,128,3,256]{3,1,2,0:T(8,128)(2,1)} %param.6) | data formatting | bytes 393216 | tf_op jit(solution)/shard_map/reshape | solution.py:430
  34.4 0.4 copy.66
  34.8 1.1 reshape.60
  35.9 0.5 broadcast.40
  36.5 1.8 %reduce.2 = bf16[128,768]{1,0:T(8,128)(2,1)S(1)} reduce(bf16[128,1,768]{2,1,0:T(2,128)(2,1)S(1)} %bitcast.57, bf16[]{:T(256)} %broadcast.40), dimensions={1}, to_apply=%bitcast.42.reduce_sub_computation | reduce | bytes 393218
  38.2 0.8 reshape.62
  39.0 11.4 %all-to-all-start = ((bf16[64,2,768]{2,1,0:T(2,128)(2,1)}), bf16[64,2,768]{2,1,0:T(2,128)(2,1)S(1)}, u32[]{:S(2)}, u32[]{:S(2)}) async-start(bf16[64,2,768]{2,1,0:T(2,128)(2,1)} %reshape.62), calls=%async_computation | async-start | bytes 393216 | tf_op jit(solution)/shard_map/all_to_all | solution.py:486
  51.0 15.7 %all-to-all-done = bf16[64,2,768]{2,1,0:T(2,128)(2,1)S(1)} async-done(((bf16[64,2,768]{2,1,0:T(2,128)(2,1)}), bf16[64,2,768]{2,1,0:T(2,128)(2,1)S(1)}, u32[]{:S(2)}, u32[]{:S(2)}) %all-to-all-start) | async-done | bytes 196640 | tf_op jit(solution)/shard_map/all_to_all | solution.py:486
  66.9 1.1 bitcast_reduce_fusion
  68.1 0.6 broadcast_in_dim.10.head_ref
  68.8 0.2 spread.1.patches_ref
  69.0 0.7 copy-done
  69.7 13.5 %all-gather.4.cloned.1.call-done = bf16[2816,1024]{1,0:T(8,128)(2,1)} async-done(((bf16[176,1024]{1,0:T(8,128)(2,1)}), bf16[2816,1024]{1,0:T(8,128)(2,1)}) %all-gather.4.cloned.1.call-update) | async-done | bytes 5767184 | tf_op jit(solution)/shard_map/all_gather | solution.py:484
  83.2 7.7 %forward.1 = (f32[128,1024]{1,0:T(8,128)}, f32[128,128]{1,0:T(8,128)}, bf16[128,1536]{1,0:T(8,128)(2,1)}, f32[8,128,128]{2,1,0:T(8,128)}, f32[128,1024]{1,0:T(8,...) custom-call(bf16[128,768]{1,0:T(8,128)(2,1)} %copy-done, bf16[16,176,1024]{2,1,0:T(8,128)(2,1)} %bitcast.47, ...), custom_call_target="tpu_custom_call" | custom-call | tf_op jit(solution)/shard_map/forward/pallas_call | solution.py:495
  90.9 10.5 %all-to-all-start.1 = ((f32[64,1,128]{2,1,0:T(1,128)}), f32[64,1,128]{2,1,0:T(1,128)S(1)}, u32[]{:S(2)}, u32[]{:S(2)}) async-start(f32[64,1,128]{2,1,0:T(1,128)} %bitcast.62), calls=%async_computation.1 | async-start | bytes 65536 | tf_op jit(solution)/shard_map/all_to_all | solution.py:526
  101.4 6.2 %before.1 = (f32[128,1024]{1,0:T(8,128)}, f32[128,512]{1,0:T(8,128)}, f32[8,128,128]{2,1,0:T(8,128)}, bf16[8,128,128]{2,1,0:T(8,128)(2,1)}, f32[128,1024]{1,0:T(8,128)}) custom-call(f32[128,1024]{1,0:T(8,128)} %get-tuple-element.28.second_in, f32[128,128]{1,0:T(8,128)} %get-tuple-element.29.second_scale_ref, f32[8,1024]{1,0:T(8,128)} %broadcast_in_dim.10.head_ref, ...), custom_call_target="tpu_custom_call" | custom-call | flops 1073741824 | bytes 8388608 | tf_op jit(solution)/shard_map/before/pallas_call | solution.py:527
  107.6 5.6 %all-to-all-done.1 = f32[64,1,128]{2,1,0:T(1,128)S(1)} async-done(((f32[64,1,128]{2,1,0:T(1,128)}), f32[64,1,128]{2,1,0:T(1,128)S(1)}, u32[]{:S(2)}, u32[]{:S(2)}) %all-to-all-start.1) | async-done | bytes 32800 | tf_op jit(solution)/shard_map/all_to_all | solution.py:526
  113.2 0.6 copy-done.1
  113.8 5.3 %backward.1 = (bf16[768,128]{1,0:T(8,128)(2,1)}, f32[1]{0:T(128)}) custom-call(s32[1]{0:T(128)} %bitcast.tile_ref, f32[64,128]{1,0:T(8,128)} %bitcast.59, f32[8,128,128]{2,1,0:T(8,128)} %get-tuple-element.32.scores_in, f32[128,512]{1,0:T(8,128)} %get-tuple-element.33.attended_in, f32[128,1024]{1,0:T(8,128)} %get-tuple-element.34.hidden_in, ...), custom_call_target="tpu_custom_call" | custom-call | tf_op jit(solution)/shard_map/backward/pallas_call | solution.py:558
  119.1 12.6 %all_to_all.28 = bf16[8,96,128]{2,1,0:T(8,128)(2,1)S(1)} all-to-all(bf16[8,96,128]{2,1,0:T(8,128)(2,1)} %bitcast.58), channel_id=1, replica_groups=mesh['zl'=2,'x'=4,'y'=8,'zh'=4,'core'=2] {'zh','core'}, dimensions={0} | all-to-all | bytes 393216 | tf_op jit(solution)/shard_map/all_to_all | solution.py:584
  131.7 4.7 %collective-permute-start = (bf16[8,48,128]{2,1,0:T(8,128)(2,1)S(1)}, bf16[8,48,128]{2,1,0:T(8,128)(2,1)S(1)}, u32[]{:S(2)}, u32[]{:S(2)}) collective-permute-start(bf16[8,48,128]{2,1,0:T(8,128)(2,1)S(1)} %get-tuple-element.42), channel_id=1, source_target_pairs={{0,1},{1,2},{2,3},{3,4},{4,5},{5,6},{6,7},{7,8},{8,9},{9,10},{10,1... | collective-permute-start | bytes 294920 | tf_op jit(solution)/shard_map/ppermute | solution.py:591
  136.4 1.9 %collective-permute-start.1 = (bf16[8,48,128]{2,1,0:T(8,128)(2,1)S(1)}, bf16[8,48,128]{2,1,0:T(8,128)(2,1)S(1)}, u32[]{:S(2)}, u32[]{:S(2)}) collective-permute-start(bf16[8,48,128]{2,1,0:T(8,128)(2,1)S(1)} %get-tuple-element.43), channel_id=1, source_target_pairs={{1,0},{2,1},{3,2},{4,3},{5,4},{6,5},{7,6},{8,7},{9,8},{10,9},{11,1... | collective-permute-start | bytes 294920 | tf_op jit(solution)/shard_map/ppermute | solution.py:592
  138.4 0.2 reshape.54
  138.7 0.3 copy.60.own_ref
  139.0 5.2 %collective-permute-done.1 = bf16[8,48,128]{2,1,0:T(8,128)(2,1)S(1)} collective-permute-done((bf16[8,48,128]{2,1,0:T(8,128)(2,1)S(1)}, bf16[8,48,128]{2,1,0:T(8,128)(2,1)S(1)}, u32[]{:S(2)}, u32[]{:S(2)}) %collective-permute-start.1) | collective-permute-done | bytes 98336 | tf_op jit(solution)/shard_map/ppermute | solution.py:592
  144.3 0.2 reshape.56
  144.7 0.3 copy.61.halo_ref
  144.9 3.1 %conv.1 = bf16[64,2,48,256]{3,2,1,0:T(8,128)(2,1)} custom-call(bf16[64,8,256]{2,1,0:T(8,128)(2,1)S(1)} %copy.60.own_ref, bf16[64,8,256]{2,1,0:T(8,128)(2,1)S(1)} %copy.61.halo_ref, bf16[384,192]{1,0:T(8,128)(2,1)S(1)} %fusion.2.kernel_ref), custom_call_target="tpu_custom_call" | custom-call | tf_op jit(solution)/shard_map/conv/pallas_call | solution.py:596
  (31 shorter events, 1.1 us)
Async XLA Ops:
  7.2 76.0 %all-gather.4.cloned.1.call-start = ((), (), s32[]{:S(2)}) async-start(), calls=%async_computation.3 | async-start | bytes 6127616 | tf_op jit(solution)/shard_map/all_gather | solution.py:484
  34.4 16.1 %copy-start.2 = (bf16[3,3,48,3]{2,3,1,0:T(4,128)(2,1)S(1)}, bf16[3,3,48,3]{2,3,1,0:T(4,128)(2,1)}, u32[]{:S(2)}) copy-start(bf16[3,3,48,3]{2,3,1,0:T(4,128)(2,1)} %param.11) | copy-start | bytes 7780
  34.8 33.3 %copy-start.3 = (f32[1024]{0:T(1024)S(1)}, f32[1024]{0:T(1024)}, u32[]{:S(2)}) copy-start(f32[1024]{0:T(1024)} %param.10) | copy-start | bytes 12292
  39.0 27.7 %all-to-all-start = ((bf16[64,2,768]{2,1,0:T(2,128)(2,1)}), bf16[64,2,768]{2,1,0:T(2,128)(2,1)S(1)}, u32[]{:S(2)}, u32[]{:S(2)}) async-start(bf16[64,2,768]{2,1,0:T(2,128)(2,1)} %reshape.62), calls=%async_computation | async-start | bytes 393216 | tf_op jit(solution)/shard_map/all_to_all | solution.py:486
  69.0 0.7 copy-start
  90.9 22.3 %all-to-all-start.1 = ((f32[64,1,128]{2,1,0:T(1,128)}), f32[64,1,128]{2,1,0:T(1,128)S(1)}, u32[]{:S(2)}, u32[]{:S(2)}) async-start(f32[64,1,128]{2,1,0:T(1,128)} %bitcast.62), calls=%async_computation.1 | async-start | bytes 65536 | tf_op jit(solution)/shard_map/all_to_all | solution.py:526
  113.2 0.6 copy-start.1
  131.7 7.3 %collective-permute-start = (bf16[8,48,128]{2,1,0:T(8,128)(2,1)S(1)}, bf16[8,48,128]{2,1,0:T(8,128)(2,1)S(1)}, u32[]{:S(2)}, u32[]{:S(2)}) collective-permute-start(bf16[8,48,128]{2,1,0:T(8,128)(2,1)S(1)} %get-tuple-element.42), channel_id=1, source_target_pairs={{0,1},{1,2},{2,3},{3,4},{4,5},{5,6},{6,7},{7,8},{8,9},{9,10},{10,1... | collective-permute-start | bytes 294920 | tf_op jit(solution)/shard_map/ppermute | solution.py:591
  136.4 7.8 %collective-permute-start.1 = (bf16[8,48,128]{2,1,0:T(8,128)(2,1)S(1)}, bf16[8,48,128]{2,1,0:T(8,128)(2,1)S(1)}, u32[]{:S(2)}, u32[]{:S(2)}) collective-permute-start(bf16[8,48,128]{2,1,0:T(8,128)(2,1)S(1)} %get-tuple-element.43), channel_id=1, source_target_pairs={{1,0},{2,1},{3,2},{4,3},{5,4},{6,5},{7,6},{8,7},{9,8},{10,9},{11,1... | collective-permute-start | bytes 294920 | tf_op jit(solution)/shard_map/ppermute | solution.py:592
Sparse Core Ops, SparseCore 0:
  32.4 50.6 all-gather.3

commit v5 on v4

--- a/solution.py
+++ b/solution.py
@@ -21,7 +21,7 @@
 IMAGE_W = 256
 TOGETHER = 4
 MIB = 2**20
-CHUNKS = 4
+CHUNKS = 2
 
 GRP = ("zl", "x")
 TILE = ("y", "zh", "core")
@@ -296,10 +296,10 @@
             grad_probs = dot_t(pick(mine, grad), value)
             probs = probs_ref[2 * pair + side]
             delta = jnp.sum(probs * grad_probs, -1, keepdims=True)
-            scores = probs * (grad_probs - delta) * HEAD_DIM ** (-0.5)
-            parts.append(dot(scores.astype(BF16), key))
+            scores = (probs * (grad_probs - delta) * HEAD_DIM ** (-0.5)).astype(BF16)
+            parts.append(dot(scores, key))
             scores_ref[2 * pair + side] = scores.T
-            probs_t_ref[2 * pair + side] = probs.T.astype(BF16)
+            probs_t_ref[2 * pair + side] = probs.astype(BF16).T
         grad_query.append(jnp.where(low, parts[0], parts[1]).astype(BF16))
     start_all(results[2:4])
     wait_all(query_copies)
@@ -376,7 +376,7 @@
         grad = (factor * attended_ref[:, at : at + 128]).astype(BF16)
         parts = []
         for side in range(2):
-            scores = (factor_line * scores_ref[2 * pair + side]).astype(BF16)
+            scores = (factor_line * scores_ref[2 * pair + side].astype(F32)).astype(BF16)
             parts.append((dot(scores, query), dot(probs_t_ref[2 * pair + side], grad)))
         for part in range(2):
             grad_proj[:, part * INNER + at : part * INNER + at + 128] = jnp.where(
@@ -529,7 +529,7 @@
         out_shape=(
             shape((ROWS, D), F32),
             shape((ROWS, INNER), F32),
-            shape((HEADS, ROWS, ROWS), F32),
+            shape((HEADS, ROWS, ROWS), BF16),
             shape((HEADS, ROWS, ROWS), BF16),
             shape((ROWS, D), F32),
         ),
@@ -541,7 +541,7 @@
             pltpu.VMEM((HEADS, ROWS, ROWS), F32),
             pltpu.VMEM((ROWS, D), F32),
             pltpu.VMEM((ROWS, INNER), F32),
-            pltpu.VMEM((HEADS, ROWS, ROWS), F32),
+            pltpu.VMEM((HEADS, ROWS, ROWS), BF16),
             pltpu.VMEM((HEADS, ROWS, ROWS), BF16),
             pltpu.VMEM((ROWS, D), F32),
             pltpu.VMEM((16, 32, D), BF16),
@@ -561,7 +561,7 @@
         in_specs=[SCALARS] + [ANYWHERE] * 10,
         out_specs=(vmem(1)[0], SCALARS),
         scratch_shapes=[
-            pltpu.VMEM((HEADS, ROWS, ROWS), F32),
+            pltpu.VMEM((HEADS, ROWS, ROWS), BF16),
             pltpu.VMEM((ROWS, INNER), F32),
             pltpu.VMEM((ROWS, D), F32),
             pltpu.VMEM((ROWS, INNER), BF16),

time: 155 us -> 155 us (level)
  no operation moved by 1% of the time
where the time goes in v5:
time: 155 us
  waiting for transfers between devices  40.1 us (26%)
  blocking collectives  35.2 us (23%)
  starting transfers between devices  28.6 us (18%)
  Pallas kernels  23 us (15%)
  between operations  14.4 us (9%)
  local copies, waits for them, and re-layouts  10.5 us (7%)
  other arithmetic  2.79 us (2%)
    all_gather x1, blocking collectives, gather_weights(): near = lax.all_gather(packed, ROW, axis=0)  22.6 us
    all_to_all x1, waiting for transfers between devices, on_device(): lax.all_to_all(patches, TILE, split_axis=1, concat_axis=0, tiled=True)  15.7 us
    all_gather x1, waiting for transfers between devices, on_device(): packed = lax.all_gather(near, ('y', 'core'), axis=0)  13.5 us
    all_to_all x1, blocking collectives, on_device(): lax.all_to_all(grad.reshape(8, PDIM // 8, ROWS), ROW, split_axis=0, conca...  12.6 us
    all_to_all x1, starting transfers between devices, on_device(): lax.all_to_all(patches, TILE, split_axis=1, concat_axis=0, tiled=True)  11.4 us
    all_to_all x1, starting transfers between devices, on_device(): lax.all_to_all(sums, TILE, split_axis=0, concat_axis=0, tiled=True)  10.5 us
    pallas_call x1, Pallas kernels, on_device(): pl.pallas_call(forward_kernel, out_shape=(shape((ROWS, D), F32), shape((R...  7.61 us
    pallas_call x1, Pallas kernels, on_device(): pl.pallas_call(before_kernel, out_shape=(shape((ROWS, D), F32), shape((RO...  6.13 us
  transfers between devices with their start and end apart: 5, of which 4 were waited for; matrix products, arithmetic and copies ran while one was open for 6% of the time, Pallas kernels for 4%

profile of v5, /device:TPU:1, one launch (start us, length us, event | category | flops | bytes accessed | tf_op | source)
XLA Modules:
  0.0 154.5 jit_solution(7408216229654744850)
XLA Ops:
  7.2 0.7 fusion.12
  7.9 0.8 fusion.7
  8.8 22.6 %all-gather = bf16[128,3072]{1,0:T(8,128)(2,1)S(1)} all-gather(bf16[16,3072]{1,0:T(8,128)(2,1)S(1)} %fusion.7), channel_id=2, replica_groups=mesh['zl'=2,'x'=4,'y'=8,'zh'=4,'core'=2] {'zh','core'}, dimensions={0}, use_global_device_ids=true | all-gather | bytes 884736 | tf_op jit(solution)/shard_map/all_gather | solution.py:469
  31.3 0.9 arrange.1
  32.3 2.1 %reshape.48 = bf16[1,8,16,3,16,16]{5,4,2,1,3,0:T(8,128)(2,1)S(1)} reshape(bf16[1,128,3,256]{3,1,2,0:T(8,128)(2,1)} %param.6) | data formatting | bytes 393216 | tf_op jit(solution)/shard_map/reshape | solution.py:430
  34.4 0.4 copy.66
  34.8 1.1 reshape.60
  35.9 0.5 broadcast.40
  36.5 1.8 %reduce.2 = bf16[128,768]{1,0:T(8,128)(2,1)S(1)} reduce(bf16[128,1,768]{2,1,0:T(2,128)(2,1)S(1)} %bitcast.57, bf16[]{:T(256)} %broadcast.40), dimensions={1}, to_apply=%bitcast.42.reduce_sub_computation | reduce | bytes 393218
  38.2 0.8 reshape.62
  39.0 11.4 %all-to-all-start = ((bf16[64,2,768]{2,1,0:T(2,128)(2,1)}), bf16[64,2,768]{2,1,0:T(2,128)(2,1)S(1)}, u32[]{:S(2)}, u32[]{:S(2)}) async-start(bf16[64,2,768]{2,1,0:T(2,128)(2,1)} %reshape.62), calls=%async_computation | async-start | bytes 393216 | tf_op jit(solution)/shard_map/all_to_all | solution.py:486
  51.0 15.7 %all-to-all-done = bf16[64,2,768]{2,1,0:T(2,128)(2,1)S(1)} async-done(((bf16[64,2,768]{2,1,0:T(2,128)(2,1)}), bf16[64,2,768]{2,1,0:T(2,128)(2,1)S(1)}, u32[]{:S(2)}, u32[]{:S(2)}) %all-to-all-start) | async-done | bytes 196640 | tf_op jit(solution)/shard_map/all_to_all | solution.py:486
  66.9 1.1 bitcast_reduce_fusion
  68.1 0.6 broadcast_in_dim.10.head_ref
  68.8 0.2 spread.1.patches_ref
  69.0 0.7 copy-done
  69.7 13.5 %all-gather.4.cloned.1.call-done = bf16[2816,1024]{1,0:T(8,128)(2,1)} async-done(((bf16[176,1024]{1,0:T(8,128)(2,1)}), bf16[2816,1024]{1,0:T(8,128)(2,1)}) %all-gather.4.cloned.1.call-update) | async-done | bytes 5767184 | tf_op jit(solution)/shard_map/all_gather | solution.py:484
  83.2 7.6 %forward.1 = (f32[128,1024]{1,0:T(8,128)}, f32[128,128]{1,0:T(8,128)}, bf16[128,1536]{1,0:T(8,128)(2,1)}, f32[8,128,128]{2,1,0:T(8,128)}, f32[128,1024]{1,0:T(8,...) custom-call(bf16[128,768]{1,0:T(8,128)(2,1)} %copy-done, bf16[16,176,1024]{2,1,0:T(8,128)(2,1)} %bitcast.47, ...), custom_call_target="tpu_custom_call" | custom-call | tf_op jit(solution)/shard_map/forward/pallas_call | solution.py:495
  90.8 10.5 %all-to-all-start.1 = ((f32[64,1,128]{2,1,0:T(1,128)}), f32[64,1,128]{2,1,0:T(1,128)S(1)}, u32[]{:S(2)}, u32[]{:S(2)}) async-start(f32[64,1,128]{2,1,0:T(1,128)} %bitcast.62), calls=%async_computation.1 | async-start | bytes 65536 | tf_op jit(solution)/shard_map/all_to_all | solution.py:526
  101.3 6.1 %before.1 = (f32[128,1024]{1,0:T(8,128)}, f32[128,512]{1,0:T(8,128)}, bf16[8,128,128]{2,1,0:T(8,128)(2,1)}, bf16[8,128,128]{2,1,0:T(8,128)(2,1)}, f32[128,1024]{1,0:T(8,128)}) custom-call(f32[128,1024]{1,0:T(8,128)} %get-tuple-element.28.second_in, f32[128,128]{1,0:T(8,128)} %get-tuple-element.29.second_scale_ref, f32[8,1024]{1,0:T(8,128)} %broadcast_in_dim.10.head_ref, ...), custom_call_target="tpu_custom_call" | custom-call | flops 1073741824 | bytes 8388608 | tf_op jit(solution)/shard_map/before/pallas_call | solution.py:527
  107.4 5.6 %all-to-all-done.1 = f32[64,1,128]{2,1,0:T(1,128)S(1)} async-done(((f32[64,1,128]{2,1,0:T(1,128)}), f32[64,1,128]{2,1,0:T(1,128)S(1)}, u32[]{:S(2)}, u32[]{:S(2)}) %all-to-all-start.1) | async-done | bytes 32800 | tf_op jit(solution)/shard_map/all_to_all | solution.py:526
  113.1 0.6 copy-done.1
  113.7 5.0 %backward.1 = (bf16[768,128]{1,0:T(8,128)(2,1)}, f32[1]{0:T(128)}) custom-call(s32[1]{0:T(128)} %bitcast.tile_ref, f32[64,128]{1,0:T(8,128)} %bitcast.59, bf16[8,128,128]{2,1,0:T(8,128)(2,1)} %get-tuple-element.32.scores_in, f32[128,512]{1,0:T(8,128)} %get-tuple-element.33.attended_in, f32[128,1024]{1,0:T(8,128)} %get-tuple-element.34.hidden_in, ...), custom_call_target="tpu_custom_call" | custom-call | tf_op jit(solution)/shard_map/backward/pallas_call | solution.py:558
  118.7 12.6 %all_to_all.28 = bf16[8,96,128]{2,1,0:T(8,128)(2,1)S(1)} all-to-all(bf16[8,96,128]{2,1,0:T(8,128)(2,1)} %bitcast.58), channel_id=1, replica_groups=mesh['zl'=2,'x'=4,'y'=8,'zh'=4,'core'=2] {'zh','core'}, dimensions={0} | all-to-all | bytes 393216 | tf_op jit(solution)/shard_map/all_to_all | solution.py:584
  131.4 4.7 %collective-permute-start = (bf16[8,48,128]{2,1,0:T(8,128)(2,1)S(1)}, bf16[8,48,128]{2,1,0:T(8,128)(2,1)S(1)}, u32[]{:S(2)}, u32[]{:S(2)}) collective-permute-start(bf16[8,48,128]{2,1,0:T(8,128)(2,1)S(1)} %get-tuple-element.42), channel_id=1, source_target_pairs={{0,1},{1,2},{2,3},{3,4},{4,5},{5,6},{6,7},{7,8},{8,9},{9,10},{10,1... | collective-permute-start | bytes 294920 | tf_op jit(solution)/shard_map/ppermute | solution.py:591
  136.0 1.9 %collective-permute-start.1 = (bf16[8,48,128]{2,1,0:T(8,128)(2,1)S(1)}, bf16[8,48,128]{2,1,0:T(8,128)(2,1)S(1)}, u32[]{:S(2)}, u32[]{:S(2)}) collective-permute-start(bf16[8,48,128]{2,1,0:T(8,128)(2,1)S(1)} %get-tuple-element.43), channel_id=1, source_target_pairs={{1,0},{2,1},{3,2},{4,3},{5,4},{6,5},{7,6},{8,7},{9,8},{10,9},{11,1... | collective-permute-start | bytes 294920 | tf_op jit(solution)/shard_map/ppermute | solution.py:592
  138.0 0.2 reshape.54
  138.4 0.3 copy.60.own_ref
  138.6 5.2 %collective-permute-done.1 = bf16[8,48,128]{2,1,0:T(8,128)(2,1)S(1)} collective-permute-done((bf16[8,48,128]{2,1,0:T(8,128)(2,1)S(1)}, bf16[8,48,128]{2,1,0:T(8,128)(2,1)S(1)}, u32[]{:S(2)}, u32[]{:S(2)}) %collective-permute-start.1) | collective-permute-done | bytes 98336 | tf_op jit(solution)/shard_map/ppermute | solution.py:592
  143.9 0.2 reshape.56
  144.3 0.3 copy.61.halo_ref
  144.6 3.1 %conv.1 = bf16[64,2,48,256]{3,2,1,0:T(8,128)(2,1)} custom-call(bf16[64,8,256]{2,1,0:T(8,128)(2,1)S(1)} %copy.60.own_ref, bf16[64,8,256]{2,1,0:T(8,128)(2,1)S(1)} %copy.61.halo_ref, bf16[384,192]{1,0:T(8,128)(2,1)S(1)} %fusion.2.kernel_ref), custom_call_target="tpu_custom_call" | custom-call | tf_op jit(solution)/shard_map/conv/pallas_call | solution.py:596
  (31 shorter events, 1.1 us)
Async XLA Ops:
  7.2 76.0 %all-gather.4.cloned.1.call-start = ((), (), s32[]{:S(2)}) async-start(), calls=%async_computation.3 | async-start | bytes 6127616 | tf_op jit(solution)/shard_map/all_gather | solution.py:484
  34.4 16.1 %copy-start.2 = (bf16[3,3,48,3]{2,3,1,0:T(4,128)(2,1)S(1)}, bf16[3,3,48,3]{2,3,1,0:T(4,128)(2,1)}, u32[]{:S(2)}) copy-start(bf16[3,3,48,3]{2,3,1,0:T(4,128)(2,1)} %param.11) | copy-start | bytes 7780
  34.8 33.3 %copy-start.3 = (f32[1024]{0:T(1024)S(1)}, f32[1024]{0:T(1024)}, u32[]{:S(2)}) copy-start(f32[1024]{0:T(1024)} %param.10) | copy-start | bytes 12292
  39.0 27.7 %all-to-all-start = ((bf16[64,2,768]{2,1,0:T(2,128)(2,1)}), bf16[64,2,768]{2,1,0:T(2,128)(2,1)S(1)}, u32[]{:S(2)}, u32[]{:S(2)}) async-start(bf16[64,2,768]{2,1,0:T(2,128)(2,1)} %reshape.62), calls=%async_computation | async-start | bytes 393216 | tf_op jit(solution)/shard_map/all_to_all | solution.py:486
  69.0 0.7 copy-start
  90.8 22.3 %all-to-all-start.1 = ((f32[64,1,128]{2,1,0:T(1,128)}), f32[64,1,128]{2,1,0:T(1,128)S(1)}, u32[]{:S(2)}, u32[]{:S(2)}) async-start(f32[64,1,128]{2,1,0:T(1,128)} %bitcast.62), calls=%async_computation.1 | async-start | bytes 65536 | tf_op jit(solution)/shard_map/all_to_all | solution.py:526
  113.1 0.6 copy-start.1
  131.4 7.3 %collective-permute-start = (bf16[8,48,128]{2,1,0:T(8,128)(2,1)S(1)}, bf16[8,48,128]{2,1,0:T(8,128)(2,1)S(1)}, u32[]{:S(2)}, u32[]{:S(2)}) collective-permute-start(bf16[8,48,128]{2,1,0:T(8,128)(2,1)S(1)} %get-tuple-element.42), channel_id=1, source_target_pairs={{0,1},{1,2},{2,3},{3,4},{4,5},{5,6},{6,7},{7,8},{8,9},{9,10},{10,1... | collective-permute-start | bytes 294920 | tf_op jit(solution)/shard_map/ppermute | solution.py:591
  136.0 7.8 %collective-permute-start.1 = (bf16[8,48,128]{2,1,0:T(8,128)(2,1)S(1)}, bf16[8,48,128]{2,1,0:T(8,128)(2,1)S(1)}, u32[]{:S(2)}, u32[]{:S(2)}) collective-permute-start(bf16[8,48,128]{2,1,0:T(8,128)(2,1)S(1)} %get-tuple-element.43), channel_id=1, source_target_pairs={{1,0},{2,1},{3,2},{4,3},{5,4},{6,5},{7,6},{8,7},{9,8},{10,9},{11,1... | collective-permute-start | bytes 294920 | tf_op jit(solution)/shard_map/ppermute | solution.py:592
Sparse Core Ops, SparseCore 0:
  32.4 50.6 all-gather.3
